TPU v7x, 128 devices: a whole 4x4x4 slice. The times are simulated.
128 devices in a mesh: len: 16 (over z, x), xs: 8 (over y, core).
Axes of the slice: x: 4, y: 4, z: 4, core: 2. Of those that a mesh axis runs over, the one named last changes fastest.
Arguments:
- right_side: float32 [3, 16, 64, 16384], P(None, None, None, ('len', 'xs')), may hold values from -19 to 19
- mass_field: float32 [16, 64, 16384], P(None, None, ('len', 'xs')), may hold values from 0.5 to 2
- span_lengths: int32 [128], replicated, may hold values from 1 to 256, 16384 in all
- stick_flags: int32 [256], replicated, may hold values from 0 to 1
- normal_load: float32 [256], replicated, may hold values from 0.5 to 4
- prior_friction: float32 [2, 256], replicated, may hold values from -4 to 4
Outputs:
- increment: float32 [3, 16, 64, 16384], P(None, None, None, ('len', 'xs'))
- residual: float32 [3, 16, 64, 16384], P(None, None, None, ('len', 'xs'))
- friction: float32 [2, 256], replicated
Inputs may be any that keep to these rules, and one draw needn't show every extreme that they name: `span_lengths`: the spans sum to 16384; the longest is exactly 256. `stick_flags`: 1 marks a sticking bearing, 0 a sliding one.
All inputs are finite; a program needn't handle non-finite values.
Results may differ from a plain program's by a relative error of at most 0.0003.
Values sent between devices are 32-bit elements; how exact they have to be, the bound alone decides.
A program may use at most 64 MiB of HBM per device.

v0:
```python
import jax
import jax.numpy as jnp
from jax import lax
from jax.sharding import PartitionSpec as P

ITERS = 3


shear_modulus = 1.0
bulk_modulus = 1.5
elastic_stiffness = 8.0
pendulum_radius = 4.0
vertical_stiffness = 5.0
static_friction = 0.6
kinetic_friction = 0.45


def extended_2(cells, sides, width):
    for axis, dim in sides:
        count = lax.axis_size(axis)
        ends = count - 1
        head = lax.slice_in_dim(cells, 0, width, axis=dim)
        tail = lax.slice_in_dim(cells, cells.shape[dim] - width, cells.shape[dim], axis=dim)
        cells = jnp.concatenate(
            [
                lax.ppermute(tail, axis, [(i, (i + 1) % count) for i in range(ends)]),
                cells,
                lax.ppermute(head, axis, [((i + 1) % count, i) for i in range(ends)]),
            ],
            axis=dim,
        )
    return cells


def window(array, anchor, extent):
    return array[
        ...,
        anchor[0] : anchor[0] + extent[0],
        anchor[1] : anchor[1] + extent[1],
        anchor[2] : anchor[2] + extent[2],
    ]


def shifted(anchor, along_dim, stride):
    moved = list(anchor)
    moved[along_dim] = moved[along_dim] + stride
    return tuple(moved)


def difference(array, anchor, extent, along_dim):
    upper = window(array, shifted(anchor, along_dim, 1), extent)
    lower = window(array, shifted(anchor, along_dim, -1), extent)
    return 0.5 * (upper - lower)


def laplace_at(padded, anchor, extent):
    total = 6.0 * window(padded, anchor, extent)
    for along_dim in range(3):
        for stride in (1, -1):
            total = total - window(padded, shifted(anchor, along_dim, stride), extent)
    return total


def pad_local(array, width):
    widths = [(0, 0)] * array.ndim
    widths[array.ndim - 3] = (width, width)
    widths[array.ndim - 2] = (width, width)
    return jnp.pad(array, widths)


def operate(field, mass_field):
    dims_of = (2, 1, 0)
    extent = field.shape[1:]
    extended = extended_2(field, ((("len", "xs"), 3),), 1)
    extended = pad_local(extended, 1)
    divergence = difference(extended[0], (1, 1, 1), extent, dims_of[0])
    for component in (1, 2):
        divergence = divergence + difference(
            extended[component], (1, 1, 1), extent, dims_of[component]
        )
    div_extended = extended_2(divergence, ((("len", "xs"), 2),), 1)
    div_extended = pad_local(div_extended, 1)
    laplacian = laplace_at(extended, (1, 1, 1), extent)
    gradient = jnp.stack(
        [difference(div_extended, (1, 1, 1), extent, dims_of[c]) for c in range(3)]
    )
    return mass_field[None] * field + shear_modulus * laplacian - bulk_modulus * gradient


def return_map(readout, stick_flags, normal_load, prior_friction):
    coeff = jnp.where(stick_flags == 1, static_friction, kinetic_friction)
    radius = coeff * normal_load
    trial = prior_friction + elastic_stiffness * readout[0:2]
    magnitude = jnp.sqrt(trial[0] * trial[0] + trial[1] * trial[1])
    friction = trial * (radius / jnp.maximum(magnitude, radius))
    horizontal = friction + normal_load / pendulum_radius * readout[0:2]
    vertical = vertical_stiffness * readout[2]
    force = jnp.concatenate([horizontal, vertical[None]], axis=0)
    return (friction, force)


def shards(right_side, mass_field, span_lengths, stick_flags, normal_load, prior_friction):
    local_across = right_side.shape[2]
    local_along = right_side.shape[3]
    bearings = 2 * span_lengths.shape[0]
    ends = jnp.cumsum(span_lengths) - 1
    along_site = jnp.repeat(ends, 2)
    across_site = jnp.tile(
        jnp.array([local_across // 4, 3 * local_across // 4], dtype=jnp.int32),
        span_lengths.shape[0],
    )
    along_start = lax.axis_index(("len", "xs")) * local_along
    along_hit = (
        lax.broadcasted_iota(jnp.int32, (local_along, bearings), 0) + along_start
        == along_site[None, :]
    ).astype(jnp.float32)
    across_hit = (
        lax.broadcasted_iota(jnp.int32, (local_across, bearings), 0) == across_site[None, :]
    ).astype(jnp.float32)
    increment = jnp.zeros_like(right_side)
    solved = right_side
    direction = right_side
    norm_now = lax.psum(jnp.sum(solved * solved), ("len", "xs"))
    for iteration in range(ITERS):
        image = operate(direction, mass_field)
        curvature = lax.psum(jnp.sum(direction * image), ("len", "xs"))
        alpha = norm_now / curvature
        increment = increment + alpha * direction
        solved = solved - alpha * image
        norm_next = lax.psum(jnp.sum(solved * solved), ("len", "xs"))
        direction = solved + norm_next / norm_now * direction
        norm_now = norm_next
    picked = jnp.einsum("csl,lb->csb", increment[:, 0], along_hit, precision=lax.Precision.HIGHEST)
    readout = lax.psum(jnp.sum(picked * across_hit[None], axis=1), ("len", "xs"))
    friction, force = return_map(readout, stick_flags, normal_load, prior_friction)
    spread = force[:, None, :] * across_hit[None]
    placed = jnp.einsum("csb,lb->csl", spread, along_hit, precision=lax.Precision.HIGHEST)
    residual = solved.at[:, 0].add(-placed)
    return (increment, residual, friction)


def solution(mesh):
    in_specs = (
        P(None, None, None, ("len", "xs")),
        P(None, None, ("len", "xs")),
        P(),
        P(),
        P(),
        P(),
    )
    out_specs = (P(None, None, None, ("len", "xs")), P(None, None, None, ("len", "xs")), P())
    return jax.shard_map(shards, mesh=mesh, in_specs=in_specs, out_specs=out_specs, check_vma=False)
```

profile of v0, /device:TPU:1, one launch (start us, length us, event | category | flops | bytes accessed | tf_op | source)
XLA Modules:
  0.0 561.3 jit_solution(11000767857912124190)
XLA Ops:
  0.6 2.6 fusion.70
  3.8 4.6 collective-permute-start
  8.9 1.9 collective-permute-start.1
  11.8 2.2 collective-permute-done.1
  14.0 1.7 copy.71
  15.7 3.8 select_maximum_fusion.4
  19.9 0.8 fusion.46
  21.0 2.0 collective-permute-start.2
  23.0 3.6 collective-permute-start.3
  26.7 3.9 multiply_reduce_fusion.5
  30.6 1.0 collective-permute-done.2
  31.6 1.2 collective-permute-done.3
  33.3 1.0 fusion.41
  34.4 1.3 multiply_reduce_fusion.4
  35.7 76.7 %all-reduce.6 = (f32[]{:T(128)}, f32[]{:T(128)}) all-reduce(f32[]{:T(128)} %get-tuple-element.45, f32[]{:T(128)} %multiply_reduce_fusion.4), channel_id=1, replica_groups=mesh['len'=16,'xs'=8] {'len','xs'}, use_global_device_ids=true, to_apply=%region_1.2 | all-reduce | flops 2 | bytes 16 | tf_op jit(solution)/shard_map/psum | solution.py:123
  113.7 3.6 multiply_reduce_fusion.3
  117.3 64.9 %psum.51 = f32[]{:T(128)} all-reduce(f32[]{:T(128)} %get-tuple-element.30), channel_id=1, replica_groups=mesh['len'=16,'xs'=8] {'len','xs'}, use_global_device_ids=true, to_apply=%region_5.6 | all-reduce | flops 1 | bytes 8 | tf_op jit(solution)/shard_map/psum | solution.py:130
  183.5 1.8 multiply_add_fusion.2
  185.3 2.3 fusion.69
  187.6 1.9 copy.82
  189.5 1.9 collective-permute-start.4
  191.4 1.9 copy.83
  193.3 2.4 collective-permute-start.5
  195.9 1.3 copy.80
  197.2 1.7 copy.84
  198.9 1.7 copy.86
  200.6 4.1 select_maximum_fusion.2
  204.9 0.7 fusion.36
  205.7 1.1 fusion.72
  206.8 1.9 collective-permute-start.6
  208.7 3.6 collective-permute-start.7
  212.4 7.8 %fusion.7 = f32[3,16,64,128]{3,2,1,0:T(8,128)} fusion(f32[3,16,64,128]{3,2,1,0:T(8,128)} %copy.80, f32[3,16,64,1]{3,2,1,0:T(8,128)} %copy.84, f32[3,16,64,1]{3,2,1,0:T(8,128)} %copy.86, f32[3,18,66,130]{3,2,1,0:T(8,128)S(1)} %select_maximum_fusion.2, f32[16,64,128]{2,1,0:T(8,128)S(1)} %copy-done.11), kind=kLoop, calls=%fused_computation.28 | loop fusion | flops 4325376 | bytes 9986048 | tf_op jit(solution)/shard_map/add | solution.py:87
  220.2 1.7 select_maximum_fusion.8
  221.9 0.6 fusion.31
  222.5 2.1 fusion.34
  224.7 0.8 copy-done.24
  225.4 1.2 multiply_reduce_fusion.2
  226.7 74.8 %psum.52 = f32[]{:T(128)} all-reduce(f32[]{:T(128)} %multiply_reduce_fusion.2), channel_id=1, replica_groups=mesh['len'=16,'xs'=8] {'len','xs'}, use_global_device_ids=true, to_apply=%region_7.8 | all-reduce | flops 1 | bytes 8 | tf_op jit(solution)/shard_map/psum | solution.py:126
  302.8 4.7 multiply_reduce_fusion.1
  307.5 62.8 %psum.53 = f32[]{:T(128)} all-reduce(f32[]{:T(128)} %get-tuple-element.28), channel_id=1, replica_groups=mesh['len'=16,'xs'=8] {'len','xs'}, use_global_device_ids=true, to_apply=%region_9.10 | all-reduce | flops 1 | bytes 8 | tf_op jit(solution)/shard_map/psum | solution.py:130
  371.6 1.7 multiply_add_fusion.1
  373.3 2.2 fusion.68
  375.5 1.9 copy.97
  377.5 2.6 collective-permute-start.9
  380.0 1.9 copy.96
  382.0 3.0 collective-permute-start.8
  385.0 2.8 copy.94
  387.8 1.7 copy.100
  389.4 1.7 copy.98
  391.1 4.3 select_maximum_fusion
  395.7 0.7 fusion.26
  396.5 1.2 fusion.71
  397.7 1.9 collective-permute-start.10
  399.6 3.9 collective-permute-start.11
  403.5 7.7 %fusion.4 = f32[3,16,64,128]{3,2,1,0:T(8,128)} fusion(f32[3,16,64,128]{3,2,1,0:T(8,128)} %copy.94, f32[3,16,64,1]{3,2,1,0:T(8,128)} %copy.98, f32[3,16,64,1]{3,2,1,0:T(8,128)} %copy.100, f32[3,18,66,130]{3,2,1,0:T(8,128)S(1)} %select_maximum_fusion, f32[16,64,128]{2,1,0:T(8,128)S(1)} %copy-done.12), kind=kLoop, calls=%fused_computation.19 | loop fusion | flops 4325376 | bytes 9986048 | tf_op jit(solution)/shard_map/add | solution.py:87
  411.1 1.7 select_maximum_fusion.6
  412.9 0.6 fusion.21
  413.5 2.1 fusion.24
  415.7 1.3 multiply_reduce_fusion
  417.2 71.9 %psum.54 = f32[]{:T(128)} all-reduce(f32[]{:T(128)} %multiply_reduce_fusion), channel_id=1, replica_groups=mesh['len'=16,'xs'=8] {'len','xs'}, use_global_device_ids=true, to_apply=%region_11.12 | all-reduce | flops 1 | bytes 8 | tf_op jit(solution)/shard_map/psum | solution.py:126
  490.4 2.1 multiply_add_fusion
  493.7 1.2 copy.109
  495.2 63.5 %psum.55 = f32[3,256]{1,0:T(4,128)S(1)} all-reduce(f32[3,256]{1,0:T(4,128)S(1)} %fusion.16), channel_id=1, replica_groups=mesh['len'=16,'xs'=8] {'len','xs'}, use_global_device_ids=true, to_apply=%region_14.15 | all-reduce | flops 768 | bytes 6144 | tf_op jit(solution)/shard_map/psum | solution.py:134
  559.7 1.3 copy.110
  (94 shorter events, 6.6 us)
Async XLA Ops:
  3.2 7.6 %copy-start.29 = (s32[2]{0:T(128)S(1)}, s32[2]{0:T(128)}, u32[]{:S(2)}) copy-start(s32[2]{0:T(128)} %constant.71.clone) | copy-start | bytes 28
  3.2 7.8 %copy-start.28 = (s32[128]{0:T(128)S(1)}, s32[128]{0:T(128)}, u32[]{:S(2)}) copy-start(s32[128]{0:T(128)} %param.11) | copy-start | bytes 1540
  3.8 7.5 %collective-permute-start = (f32[3,16,64,1]{2,1,3,0:T(8,128)S(1)}, f32[3,16,64,1]{2,1,3,0:T(8,128)S(1)}, u32[]{:S(2)}, u32[]{:S(2)}) collective-permute-start(f32[3,16,64,1]{2,1,3,0:T(8,128)S(1)} %copy.111), channel_id=1, source_target_pairs={{0,1},{1,2},{2,3},{3,4},{4,5},{5,6},{6,7},{7,8},{8,9},{9,10},{10,1... | collective-permute-start | bytes 36872 | tf_op jit(solution)/shard_map/ppermute | solution.py:26
  8.9 5.2 collective-permute-start.1
  11.3 4.4 copy-start
  11.8 7.7 %copy-start.6 = (f32[3,16,64,1]{3,2,1,0:T(8,128)}, f32[3,16,64,1]{3,2,1,0:T(8,128)S(1)}, u32[]{:S(2)}) copy-start(f32[3,16,64,1]{3,2,1,0:T(8,128)S(1)} %copy.70) | copy-start | bytes 36868
  19.9 6.8 %copy-start.8 = (f32[3,16,64,1]{3,2,1,0:T(8,128)S(1)}, f32[3,16,64,1]{3,2,1,0:T(8,128)}, u32[]{:S(2)}) copy-start(f32[3,16,64,1]{3,2,1,0:T(8,128)} %copy.71) | copy-start | bytes 36868
  20.8 6.0 %copy-start.7 = (f32[3,16,64,1]{3,2,1,0:T(8,128)S(1)}, f32[3,16,64,1]{3,2,1,0:T(8,128)}, u32[]{:S(2)}) copy-start(f32[3,16,64,1]{3,2,1,0:T(8,128)} %copy-done.6) | copy-start | bytes 36868
  20.8 6.0 %copy-start.10 = (f32[16,64,128]{2,1,0:T(8,128)S(1)}, f32[16,64,128]{2,1,0:T(8,128)}, u32[]{:S(2)}) copy-start(f32[16,64,128]{2,1,0:T(8,128)} %param.10) | copy-start | bytes 1572868
  21.0 10.6 %collective-permute-start.2 = (f32[16,64,1]{2,1,0:T(8,128)S(1)}, f32[16,64,1]{2,1,0:T(8,128)S(1)}, u32[]{:S(2)}, u32[]{:S(2)}) collective-permute-start(f32[16,64,1]{2,1,0:T(8,128)S(1)} %get-tuple-element.60), channel_id=1, source_target_pairs={{1,0},{2,1},{3,2},{4,3},{5,4},{6,5},{7,6},{8,7},{9,8},{10,9},{11,1... | collective-permute-start | bytes 12296 | tf_op jit(solution)/shard_map/ppermute | solution.py:28
  23.0 9.8 %collective-permute-start.3 = (f32[16,64,1]{2,1,0:T(8,128)S(1)}, f32[16,64,1]{2,1,0:T(8,128)S(1)}, u32[]{:S(2)}, u32[]{:S(2)}) collective-permute-start(f32[16,64,1]{2,1,0:T(8,128)S(1)} %get-tuple-element.59), channel_id=1, source_target_pairs={{0,1},{1,2},{2,3},{3,4},{4,5},{5,6},{6,7},{7,8},{8,9},{9,10},{10,1... | collective-permute-start | bytes 12296 | tf_op jit(solution)/shard_map/ppermute | solution.py:26
  34.4 1.3 copy-start.19
  34.4 1.3 copy-start.20
  34.4 1.3 copy-start.21
  189.5 7.7 %collective-permute-start.4 = (f32[3,16,64,1]{2,1,3,0:T(8,128)S(1)}, f32[3,16,64,1]{2,1,3,0:T(8,128)S(1)}, u32[]{:S(2)}, u32[]{:S(2)}) collective-permute-start(f32[3,16,64,1]{2,1,3,0:T(8,128)S(1)} %copy.82), channel_id=1, source_target_pairs={{0,1},{1,2},{2,3},{3,4},{4,5},{5,6},{6,7},{7,8},{8,9},{9,10},{10,1... | collective-permute-start | bytes 36872 | tf_op jit(solution)/shard_map/ppermute | solution.py:26
  193.3 5.5 collective-permute-start.5
  205.7 6.7 %copy-start.11 = (f32[16,64,128]{2,1,0:T(8,128)S(1)}, f32[16,64,128]{2,1,0:T(8,128)}, u32[]{:S(2)}) copy-start(f32[16,64,128]{2,1,0:T(8,128)} %param.10) | copy-start | bytes 1572868
  206.8 13.4 %collective-permute-start.6 = (f32[16,64,1]{2,1,0:T(8,128)}, f32[16,64,1]{2,1,0:T(8,128)}, u32[]{:S(2)}, u32[]{:S(2)}) collective-permute-start(f32[16,64,1]{2,1,0:T(8,128)} %get-tuple-element.58), channel_id=1, source_target_pairs={{1,0},{2,1},{3,2},{4,3},{5,4},{6,5},{7,6},{8,7},{9,8},{10,9},{11,1... | collective-permute-start | bytes 12296 | tf_op jit(solution)/shard_map/ppermute | solution.py:28
  208.7 11.4 %collective-permute-start.7 = (f32[16,64,1]{2,1,0:T(8,128)}, f32[16,64,1]{2,1,0:T(8,128)}, u32[]{:S(2)}, u32[]{:S(2)}) collective-permute-start(f32[16,64,1]{2,1,0:T(8,128)} %get-tuple-element.57), channel_id=1, source_target_pairs={{0,1},{1,2},{2,3},{3,4},{4,5},{5,6},{6,7},{7,8},{8,9},{9,10},{10,1... | collective-permute-start | bytes 12296 | tf_op jit(solution)/shard_map/ppermute | solution.py:26
  222.5 2.1 copy-start.22
  222.5 2.1 copy-start.23
  222.5 2.9 copy-start.5
  224.6 0.8 copy-start.24
  373.3 2.2 copy-start.1
  377.5 10.3 %collective-permute-start.9 = (f32[3,16,64,1]{2,1,3,0:T(8,128)S(1)}, f32[3,16,64,1]{2,1,3,0:T(8,128)S(1)}, u32[]{:S(2)}, u32[]{:S(2)}) collective-permute-start(f32[3,16,64,1]{2,1,3,0:T(8,128)S(1)} %copy.97), channel_id=1, source_target_pairs={{1,0},{2,1},{3,2},{4,3},{5,4},{6,5},{7,6},{8,7},{9,8},{10,9},{11,1... | collective-permute-start | bytes 36872 | tf_op jit(solution)/shard_map/ppermute | solution.py:28
  382.0 7.5 %collective-permute-start.8 = (f32[3,16,64,1]{2,1,3,0:T(8,128)S(1)}, f32[3,16,64,1]{2,1,3,0:T(8,128)S(1)}, u32[]{:S(2)}, u32[]{:S(2)}) collective-permute-start(f32[3,16,64,1]{2,1,3,0:T(8,128)S(1)} %copy.96), channel_id=1, source_target_pairs={{0,1},{1,2},{2,3},{3,4},{4,5},{5,6},{6,7},{7,8},{8,9},{9,10},{10,1... | collective-permute-start | bytes 36872 | tf_op jit(solution)/shard_map/ppermute | solution.py:26
  396.5 7.0 %copy-start.12 = (f32[16,64,128]{2,1,0:T(8,128)S(1)}, f32[16,64,128]{2,1,0:T(8,128)}, u32[]{:S(2)}) copy-start(f32[16,64,128]{2,1,0:T(8,128)} %param.10) | copy-start | bytes 1572868
  397.7 13.4 %collective-permute-start.10 = (f32[16,64,1]{2,1,0:T(8,128)}, f32[16,64,1]{2,1,0:T(8,128)}, u32[]{:S(2)}, u32[]{:S(2)}) collective-permute-start(f32[16,64,1]{2,1,0:T(8,128)} %get-tuple-element.56), channel_id=1, source_target_pairs={{1,0},{2,1},{3,2},{4,3},{5,4},{6,5},{7,6},{8,7},{9,8},{10,9},{11,1... | collective-permute-start | bytes 12296 | tf_op jit(solution)/shard_map/ppermute | solution.py:28
  399.6 11.5 %collective-permute-start.11 = (f32[16,64,1]{2,1,0:T(8,128)}, f32[16,64,1]{2,1,0:T(8,128)}, u32[]{:S(2)}, u32[]{:S(2)}) collective-permute-start(f32[16,64,1]{2,1,0:T(8,128)} %get-tuple-element.55), channel_id=1, source_target_pairs={{0,1},{1,2},{2,3},{3,4},{4,5},{5,6},{6,7},{7,8},{8,9},{9,10},{10,1... | collective-permute-start | bytes 12296 | tf_op jit(solution)/shard_map/ppermute | solution.py:26
  412.8 2.8 copy-start.3
  413.5 3.5 copy-start.13
  413.5 3.5 copy-start.15
  413.5 2.2 copy-start.2
  415.6 1.4 copy-start.17
  490.3 2.1 copy-start.4
  490.3 2.3 copy-start.9
  490.4 2.4 copy-start.14
  490.4 2.6 copy-start.16
  490.4 2.7 copy-start.18
  493.6 65.1 %copy-start.25 = (f32[2,256]{1,0:T(2,128)S(1)}, f32[2,256]{1,0:T(2,128)}, u32[]{:S(2)}) copy-start(f32[2,256]{1,0:T(2,128)} %param.14) | copy-start | bytes 6148
  493.6 65.1 %copy-start.26 = (f32[256]{0:T(256)S(1)}, f32[256]{0:T(256)}, u32[]{:S(2)}) copy-start(f32[256]{0:T(256)} %param.13) | copy-start | bytes 3076
  493.7 65.1 %copy-start.27 = (s32[256]{0:T(256)S(1)}, s32[256]{0:T(256)}, u32[]{:S(2)}) copy-start(s32[256]{0:T(256)} %param.12) | copy-start | bytes 3076
where the time goes:
time: 570 us; the launch traced here: 561 us
  blocking collectives  414 us (73%)
  other arithmetic  63.3 us (11%)
  local copies, waits for them, and re-layouts  36.9 us (6%)
  starting transfers between devices  33.4 us (6%)
  between operations  8.1 us (1%)
    psum x2, blocking collectives, shards(): curvature = lax.psum(jnp.sum(direction * image), ('len', 'xs'))  147 us
    psum x2, blocking collectives, shards(): norm_next = lax.psum(jnp.sum(solved * solved), ('len', 'xs'))  128 us
    psum x1, blocking collectives, shards(): norm_now = lax.psum(jnp.sum(solved * solved), ('len', 'xs'))  76.7 us
    psum x1, blocking collectives, shards(): lax.psum(jnp.sum(picked * across_hit[None], axis=1), ('len', 'xs'))  63.5 us
    ppermute x6, starting transfers between devices, extended_2(): lax.ppermute(tail, axis, [(i, (i + 1) % count) for i in range(ends)])  20.7 us
    concatenate x6, other arithmetic, extended_2(): jnp.concatenate([lax.ppermute(tail, axis, [(i, (i + 1) % count) for i in...  16.2 us
    add x2, other arithmetic, operate(): mass_field[None] * field + shear_modulus * laplacian  15.4 us
    slice x8, local copies, waits for them, and re-layouts, extended_2(): lax.slice_in_dim(cells, cells.shape[dim] - width, cells.shape[dim], axis=...  13.4 us
  transfers between devices with their start and end apart: 12, of which 3 were waited for; matrix products, arithmetic and copies ran while one was open for 6% of the time, Pallas kernels for 0%

commit v1 on v0

v1 whole, which is shorter than its diff:
```python
import jax
import jax.numpy as jnp
from jax import lax
from jax.experimental import pallas as pl
from jax.experimental.pallas import tpu as pltpu
from jax.sharding import PartitionSpec as P

shear_modulus = 1.0
bulk_modulus = 1.5
elastic_stiffness = 8.0
pendulum_radius = 4.0
vertical_stiffness = 5.0
static_friction = 0.6
kinetic_friction = 0.45

DEPTH = 16
NS = 64
LANES = 128
PITCH = NS + 8
PADDED = (DEPTH + 2) * PITCH
HALO = 6
MASS_HALO = 4
EDGE = 6
STRIP = 24
PAIRS = DEPTH * NS // LANES
STRIP_ROWS = (PAIRS + 2) * STRIP
MESSAGE = (3 * HALO + MASS_HALO) * PAIRS
PARTIALS = 24

MESH = pl.DeviceIdType.MESH
HIGHEST = lax.Precision.HIGHEST
F32 = jnp.float32


def two_sum(a, b):
    s = a + b
    t = s - a
    return s, (a - (s - t)) + (b - t)


def fold(block):
    return jnp.sum(block.reshape(block.shape[0] // 8, 8, LANES), axis=0)


def bearing_ends(spans):
    piers = spans.shape[1]
    upto = (
        lax.broadcasted_iota(jnp.int32, (piers, 2 * piers), 0)
        <= lax.broadcasted_iota(jnp.int32, (piers, 2 * piers), 1) // 2
    ).astype(F32)
    return (
        jnp.dot(
            jnp.broadcast_to(spans.astype(F32), (8, piers)),
            upto,
            precision=HIGHEST,
            preferred_element_type=F32,
        )[0:1]
        - 1.0
    )


def bearing_hits(ends, start):
    bearings = ends.shape[1]
    along = lax.broadcasted_iota(jnp.int32, (LANES, bearings), 0) + start
    side = lax.rem(lax.broadcasted_iota(jnp.int32, (LANES, bearings), 1), 2)
    here = along.astype(F32) == ends
    return [jnp.where(here & (side == s), 1.0, 0.0).astype(F32) for s in range(2)]


def krylov_kernel(
    sizes,
    b_ref,
    mass_ref,
    spans_ref,
    out1_ref,
    out2_ref,
    out3_ref,
    sums_ref,
    v,
    mass,
    w,
    sv,
    sm,
    sw,
    valid,
    send_left,
    send_right,
    from_left,
    from_right,
    part_a,
    part_b,
    slots_a,
    slots_b,
    in_sem,
    halo_send,
    halo_recv,
    a_send,
    a_recv,
    b_send,
    b_recv,
):
    len_size, xs_size = sizes
    count = len_size * xs_size
    at_len, at_xs = lax.axis_index("len"), lax.axis_index("xs")
    me = at_len * xs_size + at_xs
    left, right = lax.rem(me + count - 1, count), lax.rem(me + 1, count)
    place = lambda i: (i // xs_size, lax.rem(i, xs_size))
    group_a = [(at_len, lax.rem(at_xs + k, xs_size)) for k in range(1, xs_size)]
    group_b = [(lax.rem(at_len + k, len_size), at_xs) for k in range(1, len_size)]

    barrier = pltpu.get_barrier_semaphore()
    partners = [place(left), place(right)] + group_a + group_b
    for partner in partners:
        pl.semaphore_signal(barrier, inc=1, device_id=partner, device_id_type=MESH)

    def load(d, carry):
        for c in range(3):
            pltpu.make_async_copy(
                b_ref.at[c, pl.ds(d * NS, NS)],
                v.at[0, c, pl.ds((d + 1) * PITCH, NS)],
                in_sem.at[c],
            ).start()
        return carry

    lax.fori_loop(0, DEPTH, load, 0)
    pltpu.make_async_copy(mass_ref, mass, in_sem.at[3]).start()

    def guard(d, carry):
        row = (d + 1) * PITCH + NS
        for c in range(3):
            for k in range(3):
                v[k, c, pl.ds(row, 8)] = jnp.zeros((8, LANES), F32)
        w[pl.ds(row, 8)] = jnp.zeros((8, LANES), F32)
        return carry

    lax.fori_loop(0, DEPTH, guard, 0)

    for start in (0, (DEPTH + 1) * PITCH):
        for c in range(3):
            for k in range(3):
                v[k, c, pl.ds(start, PITCH)] = jnp.zeros((PITCH, LANES), F32)
        w[pl.ds(start, PITCH)] = jnp.zeros((PITCH, LANES), F32)
    for start in (0, (PAIRS + 1) * STRIP):
        for side in range(2):
            sw[side, pl.ds(start, STRIP)] = jnp.zeros((STRIP, LANES), F32)
            for c in range(3):
                for k in range(3):
                    sv[k, side, c, pl.ds(start, STRIP)] = jnp.zeros((STRIP, LANES), F32)

    has_left = jnp.where(me > 0, 1.0, 0.0).astype(F32)
    has_right = jnp.where(me < count - 1, 1.0, 0.0).astype(F32)
    row = lax.broadcasted_iota(jnp.int32, (STRIP, LANES), 0)
    valid[0] = jnp.where(row < HALO, has_left, 1.0)
    valid[1] = jnp.where(row >= 2 * EDGE, has_right, 1.0)

    for c in range(4):
        if c < 3:
            pltpu.make_async_copy(
                b_ref.at[c], v.at[0, c, pl.ds(0, DEPTH * NS)], in_sem.at[c]
            ).wait()
        else:
            pltpu.make_async_copy(mass_ref, mass, in_sem.at[3]).wait()
        width = HALO if c < 3 else MASS_HALO

        def edges(t, carry, c=c, width=width):
            if c < 3:
                tile = jnp.concatenate(
                    [v[0, c, pl.ds((2 * t + 1 + i) * PITCH, NS)] for i in range(2)], axis=0
                )
            else:
                tile = mass[pl.ds(t * LANES, LANES)]
            turned = tile.T
            strip = (t + 1) * STRIP
            if c < 3:
                sv[0, 0, c, pl.ds(strip + HALO, 2 * EDGE)] = turned[: 2 * EDGE]
                sv[0, 1, c, pl.ds(strip, 2 * EDGE)] = turned[LANES - 2 * EDGE :]
            else:
                sm[0, pl.ds(strip + HALO, 2 * EDGE)] = turned[: 2 * EDGE]
                sm[1, pl.ds(strip, 2 * EDGE)] = turned[LANES - 2 * EDGE :]
            send_left[pl.ds(c * HALO * PAIRS + t, width, stride=PAIRS), :] = turned[:width]
            send_right[pl.ds(c * HALO * PAIRS + t, width, stride=PAIRS), :] = turned[
                LANES - width :
            ]
            return carry

        lax.fori_loop(0, PAIRS, edges, 0)

    pl.semaphore_wait(barrier, len(partners))
    halos = [
        pltpu.make_async_remote_copy(
            src_ref=send_left,
            dst_ref=from_right,
            send_sem=halo_send.at[0],
            recv_sem=halo_recv.at[0],
            device_id=place(left),
            device_id_type=MESH,
        ),
        pltpu.make_async_remote_copy(
            src_ref=send_right,
            dst_ref=from_left,
            send_sem=halo_send.at[1],
            recv_sem=halo_recv.at[1],
            device_id=place(right),
            device_id_type=MESH,
        ),
    ]
    for copy in halos:
        copy.start()

    def main_divergence(k):
        def body(d, carry):
            base = (d + 1) * PITCH
            first = v[k, 0, pl.ds(base, NS)]
            along = pltpu.roll(first, LANES - 1, 1) - pltpu.roll(first, 1, 1)
            across = v[k, 1, pl.ds(base + 1, NS)] - v[k, 1, pl.ds(base - 1, NS)]
            depth = v[k, 2, pl.ds(base + PITCH, NS)] - v[k, 2, pl.ds(base - PITCH, NS)]
            w[pl.ds(base, NS)] = (0.25 * bulk_modulus) * (along + across + depth)
            return carry

        lax.fori_loop(0, DEPTH, body, 0)

    def main_image(k, dots):
        zero = jnp.zeros((8, LANES), F32)

        def body(d, sums):
            base = (d + 1) * PITCH
            heavy = mass[pl.ds(d * NS, NS)] + 6.0
            terms = [zero] * len(dots)
            for c in range(3):
                here = v[k, c, pl.ds(base, NS)]
                image = heavy * here
                image = image - (v[k, c, pl.ds(base + 1, NS)] + v[k, c, pl.ds(base - 1, NS)])
                image = image - (
                    v[k, c, pl.ds(base + PITCH, NS)] + v[k, c, pl.ds(base - PITCH, NS)]
                )
                if c == 0:
                    local = w[pl.ds(base, NS)]
                    image = image - (
                        pltpu.roll(here + local, LANES - 1, 1) + pltpu.roll(here - local, 1, 1)
                    )
                else:
                    step = 1 if c == 1 else PITCH
                    image = image - (pltpu.roll(here, LANES - 1, 1) + pltpu.roll(here, 1, 1))
                    image = image - (w[pl.ds(base + step, NS)] - w[pl.ds(base - step, NS)])
                if k < 2:
                    v[k + 1, c, pl.ds(base, NS)] = image
                else:
                    out3_ref[c, pl.ds(d * NS, NS)] = image
                for n, kind in enumerate(dots):
                    terms[n] = terms[n] + fold(
                        {"vv": here * here, "vi": here * image, "ii": image * image}[kind]
                    )
            return tuple(s + t for s, t in zip(sums, terms))

        return lax.fori_loop(0, DEPTH, body, (zero,) * len(dots))

    main_divergence(0)
    mu0, mu1, mu2 = main_image(0, ("vv", "vi", "ii"))
    main_divergence(1)
    mu3, mu4 = main_image(1, ("vi", "ii"))
    main_divergence(2)
    (mu5,) = main_image(2, ("vi",))
    lane = lax.broadcasted_iota(jnp.int32, (8, LANES), 1)
    inner = (lane >= EDGE) & (lane < LANES - EDGE)
    moments = tuple(jnp.where(inner, mu, 0.0) for mu in (mu0, mu1, mu2, mu3, mu4, mu5))

    for copy in halos:
        copy.wait_recv()
    for c in range(4):
        width = HALO if c < 3 else MASS_HALO

        def unpack(t, carry, c=c, width=width):
            strip = (t + 1) * STRIP
            rows = pl.ds(c * HALO * PAIRS + t, width, stride=PAIRS)
            before = from_left[rows, :] * has_left
            after = from_right[rows, :] * has_right
            if c < 3:
                sv[0, 0, c, pl.ds(strip, width)] = before
                sv[0, 1, c, pl.ds(strip + 2 * EDGE, width)] = after
            else:
                sm[0, pl.ds(strip + HALO - width, width)] = before
                sm[1, pl.ds(strip + 2 * EDGE, width)] = after
            return carry

        lax.fori_loop(0, PAIRS, unpack, 0)

    half = LANES // 2

    def low(n):
        return lax.broadcasted_iota(jnp.int32, (n, LANES), 1) < half

    def across_pair(x):
        at = lax.rem(lax.broadcasted_iota(jnp.int32, x.shape, 1), half)
        after = jnp.where(at == half - 1, 0.0, pltpu.roll(x, LANES - 1, 1))
        before = jnp.where(at == 0, 0.0, pltpu.roll(x, 1, 1))
        return after, before

    def depth_diff(ref, base, n):
        x = ref[pl.ds(base, n)]
        up, down = ref[pl.ds(base + STRIP, n)], ref[pl.ds(base - STRIP, n)]
        return pltpu.roll(jnp.where(low(n), up - x, x - down), half, 1)

    def depth_sum(x, ref, base, n):
        up, down = ref[pl.ds(base + STRIP, n)], ref[pl.ds(base - STRIP, n)]
        return pltpu.roll(x + jnp.where(low(n), up, down), half, 1)

    for k, n in ((0, 16), (1, 16), (2, 8)):

        def strip_divergence(i, carry, k=k, n=n):
            side, t = i // PAIRS, lax.rem(i, PAIRS)
            at = 2 * k + 1
            base = (t + 1) * STRIP + at
            first = sv.at[k, side, 0]
            along = first[pl.ds(base + 1, n)] - first[pl.ds(base - 1, n)]
            after, before = across_pair(sv[k, side, 1, pl.ds(base, n)])
            depth = depth_diff(sv.at[k, side, 2], base, n)
            sw[side, pl.ds(base, n)] = (
                (0.25 * bulk_modulus)
                * (along + (after - before) + depth)
                * valid[side, pl.ds(at, n)]
            )
            return carry

        lax.fori_loop(0, 2 * PAIRS, strip_divergence, 0)

        def strip_image(i, sums, k=k, n=n):
            side, t = i // PAIRS, lax.rem(i, PAIRS)
            at = 2 * k + 2
            base = (t + 1) * STRIP + at
            heavy = sm[side, pl.ds(base, n)] + 6.0
            sw_side = sw.at[side]
            local = sw_side[pl.ds(base, n)]
            for c in range(3):
                ref = sv.at[k, side, c]
                here = ref[pl.ds(base, n)]
                image = heavy * here - (ref[pl.ds(base + 1, n)] + ref[pl.ds(base - 1, n)])
                after, before = across_pair(here)
                image = image - (after + before) - depth_sum(here, ref, base, n)
                if c == 0:
                    image = image - (sw_side[pl.ds(base + 1, n)] - sw_side[pl.ds(base - 1, n)])
                elif c == 1:
                    after, before = across_pair(local)
                    image = image - (after - before)
                else:
                    image = image - depth_diff(sw_side, base, n)
                sv[k + 1, side, c, pl.ds(base, n)] = image * valid[side, pl.ds(at, n)]
            return sums

        lax.fori_loop(0, 2 * PAIRS, strip_image, 0)

    def strip_dots(i, sums):
        side, t = i // PAIRS, lax.rem(i, PAIRS)
        base = (t + 1) * STRIP + HALO
        mine = lax.broadcasted_iota(jnp.int32, (8, LANES), 0) < EDGE
        sums = list(sums)
        for c in range(3):
            x = [jnp.where(mine, sv[k, side, c, pl.ds(base, 8)], 0.0) for k in range(4)]
            for n, (p, q) in enumerate(((0, 0), (0, 1), (1, 1), (1, 2), (2, 2), (2, 3))):
                sums[n] = sums[n] + x[p] * x[q]
        return tuple(sums)

    zero = jnp.zeros((8, LANES), F32)
    strips = lax.fori_loop(0, 2 * PAIRS, strip_dots, (zero,) * 6)

    lanes = lax.broadcasted_iota(jnp.int32, (LANES, LANES), 1)
    outer = (lanes < EDGE) | (lanes >= LANES - EDGE)

    def merge(k, c, t):
        base = (t + 1) * STRIP + EDGE
        rows = jnp.concatenate(
            [
                sv[k, 0, c, pl.ds(base, 8)],
                jnp.zeros((LANES - 16, LANES), F32),
                sv[k, 1, c, pl.ds(base - 2, 8)],
            ],
            axis=0,
        ).T
        out = (out1_ref, out2_ref, out3_ref)[k - 1]
        if k < 3:
            main = jnp.concatenate(
                [v[k, c, pl.ds((2 * t + 1 + i) * PITCH, NS)] for i in range(2)], axis=0
            )
        else:
            main = out[c, pl.ds(t * LANES, LANES)]
        out[c, pl.ds(t * LANES, LANES)] = jnp.where(outer, rows, main)

    for k in (1, 2):
        for c in (0, 1):
            merge(k, c, 0)

    head, rest = [], []
    for total in range(6):
        hi, lo = two_sum(moments[total], strips[total])
        for shift in (4, 2, 1):
            hi, more = two_sum(hi, pltpu.roll(hi, shift, 0))
            lo = lo + pltpu.roll(lo, shift, 0) + more
        head.append(hi[0:1])
        rest.append(lo[0:1])
    hits = bearing_hits(bearing_ends(spans_ref[...]), me * LANES)
    site = jnp.zeros((8, hits[0].shape[1]), F32)
    for s, across in ((0, NS // 4), (1, 3 * NS // 4)):
        rows = [v[0, c, pl.ds(PITCH + across, 1)] for c in (0, 1)]
        rows += [out1_ref[c, pl.ds(across, 1)] for c in (0, 1)]
        rows += [out2_ref[c, pl.ds(across, 1)] for c in (0, 1)]
        rows += [jnp.zeros((2, LANES), F32)]
        site = site + jnp.dot(
            jnp.concatenate(rows, axis=0),
            hits[s],
            precision=HIGHEST,
            preferred_element_type=F32,
        )
    halves = [site[:, :LANES], site[:, LANES:]]
    part_a[...] = jnp.concatenate(
        head
        + [halves[0][0:2]]
        + rest
        + [halves[1][0:2]]
        + [halves[0][2:4], halves[1][2:4], halves[0][4:6], halves[1][4:6]],
        axis=0,
    )

    def exchange(source, slots, partners, own, send_sems, recv_sems):
        copies = []
        for k, partner in enumerate(partners):
            copy = pltpu.make_async_remote_copy(
                src_ref=source,
                dst_ref=slots.at[own],
                send_sem=send_sems.at[k],
                recv_sem=recv_sems.at[k],
                device_id=partner,
                device_id_type=MESH,
            )
            copy.start()
            copies.append(copy)
        slots[own] = source[...]
        return copies

    def total(slots, number):
        parts = [(slots[i, 0:8], slots[i, 8:16], slots[i, 16:]) for i in range(number)]
        while len(parts) > 1:
            merged = []
            for i in range(0, len(parts) - 1, 2):
                hi, more = two_sum(parts[i][0], parts[i + 1][0])
                merged.append(
                    (hi, parts[i][1] + parts[i + 1][1] + more, parts[i][2] + parts[i + 1][2])
                )
            if len(parts) % 2:
                merged.append(parts[-1])
            parts = merged
        return jnp.concatenate(parts[0], axis=0)

    copies_a = exchange(part_a, slots_a, group_a, at_xs, a_send, a_recv)

    def merge_rest(t, carry, ks=(1,)):
        for k in ks:
            for c in range(3):
                merge(k, c, t)
        return carry

    lax.fori_loop(1, PAIRS, merge_rest, 0)
    merge(1, 2, 0)
    for copy in copies_a:
        copy.wait_recv()
    part_b[...] = total(slots_a, xs_size)
    copies_b = exchange(part_b, slots_b, group_b, at_len, b_send, b_recv)

    def merge_last(t, carry):
        for k in (2, 3):
            for c in range(3):
                merge(k, c, t)
        return carry

    lax.fori_loop(1, PAIRS, merge_last, 0)
    merge(2, 2, 0)
    for c in range(3):
        merge(3, c, 0)
    for copy in copies_b:
        copy.wait_recv()
    sums_ref[...] = total(slots_b, len_size)
    for copy in halos + copies_a + copies_b:
        copy.wait_send()


def steps(sums):
    hi, lo = sums[0:8], sums[8:16]
    for shift in (64, 32, 16, 8, 4, 2, 1):
        hi, more = two_sum(hi, pltpu.roll(hi, shift, 1))
        lo = lo + pltpu.roll(lo, shift, 1) + more
    hi, lo = two_sum(hi, lo)
    theta = jnp.round(hi[1:2] / hi[0:1] * 64.0) * (1.0 / 64.0)
    central = [hi[0:1]]
    for order in range(5):
        n = 5 - order
        big = hi[:n] * 4097.0
        upper = big - (big - hi[:n])
        lower = hi[:n] - upper
        value, more = two_sum(hi[1 : n + 1], -theta * upper)
        value, extra = two_sum(value, -theta * lower)
        low_part = lo[1 : n + 1] - theta * lo[:n] + (more + extra)
        hi, lo = two_sum(value, low_part)
        central.append(hi[0:1])
    scale = 1.0 / central[0]
    c = [x * scale for x in central]
    c1 = [c[i + 1] + theta * c[i] for i in range(5)]

    def form(p, moments):
        terms = None
        for i in range(len(p)):
            for j in range(i, len(p)):
                term = (1.0 if i == j else 2.0) * (p[i] * p[j]) * moments[i + j]
                terms = term if terms is None else terms + term
        return terms

    one, zero = jnp.ones_like(theta), jnp.zeros_like(theta)
    left, ahead, norm = [one], [one], c[0]
    increment = [zero, zero, zero]
    for iteration in range(3):
        alpha = norm / form(ahead, c1)
        increment = [
            x + alpha * ahead[i] if i < len(ahead) else x for i, x in enumerate(increment)
        ]
        image = [theta * x for x in ahead] + [zero]
        image = [image[i] + (ahead[i - 1] if i else zero) for i in range(len(image))]
        left = left + [zero]
        left = [x - alpha * y for x, y in zip(left, image)]
        if iteration < 2:
            after = form(left, c)
            beta = after / norm
            ahead = ahead + [zero]
            ahead = [x + beta * y for x, y in zip(left, ahead)]
            norm = after
    x0, x1, x2 = increment
    r0, r1, r2, r3 = left
    increment = (x0 - theta * (x1 - theta * x2), x1 - 2.0 * theta * x2, x2)
    solved = (
        r0 - theta * (r1 - theta * (r2 - theta * r3)),
        r1 - theta * (2.0 * r2 - 3.0 * theta * r3),
        r2 - 3.0 * theta * r3,
        r3,
    )
    return increment, solved


def finish_kernel(
    b_ref,
    v1_ref,
    v2_ref,
    v3_ref,
    sums_ref,
    spans_ref,
    stick_ref,
    load_ref,
    prior_ref,
    inc_ref,
    res_ref,
    friction_ref,
    b,
    x,
    r,
    in_sem,
    out_sem,
):
    loads = [pltpu.make_async_copy(b_ref.at[c], b.at[c], in_sem.at[c]) for c in range(3)]
    for copy in loads:
        copy.start()
    me = lax.axis_index("len") * lax.axis_size("xs") + lax.axis_index("xs")
    sums = sums_ref[...]
    (x0, x1, x2), (r0, r1, r2, r3) = steps(sums)

    def site(first, second):
        return jnp.concatenate([sums[first : first + 2], sums[second : second + 2]], axis=1)

    wide = lambda a: jnp.concatenate([a, a], axis=1)
    readout = wide(x0) * site(6, 14) + wide(x1) * site(16, 18) + wide(x2) * site(20, 22)
    radius = jnp.where(stick_ref[...] == 1, static_friction, kinetic_friction) * load_ref[...]
    trial = prior_ref[...] + elastic_stiffness * readout
    magnitude = jnp.sqrt(trial[0:1] * trial[0:1] + trial[1:2] * trial[1:2])
    friction = trial * (radius / jnp.maximum(magnitude, radius))
    friction_ref[...] = friction
    force = friction + load_ref[...] / pendulum_radius * readout
    bearings = force.shape[1]
    rows = jnp.concatenate(
        [force, jnp.ones((1, bearings), F32), jnp.zeros((5, bearings), F32)], axis=0
    )
    hits = bearing_hits(bearing_ends(spans_ref[...]), me * LANES)
    placed = [
        lax.dot_general(
            rows,
            hit,
            (((1,), (1,)), ((), ())),
            precision=HIGHEST,
            preferred_element_type=F32,
        )
        for hit in hits
    ]

    chunk = DEPTH * NS // 2
    stores = []
    for c in range(3):
        loads[c].wait()
        for part in range(2):

            def body(i, carry, c=c, part=part):
                at = pl.ds(pl.multiple_of(part * chunk + i * NS, NS), NS)
                p0, p1, p2, p3 = b[c, at], v1_ref[c, at], v2_ref[c, at], v3_ref[c, at]
                x[c, at] = x0 * p0 + x1 * p1 + x2 * p2
                r[c, at] = r0 * p0 + r1 * p1 + r2 * p2 + r3 * p3
                return carry

            lax.fori_loop(0, chunk // NS, body, 0)
            if part == 0:
                for s, across in ((0, NS // 4), (1, 3 * NS // 4)):
                    at = pl.ds(across, 1)
                    if c < 2:
                        drop = placed[s][c : c + 1]
                    else:
                        drop = vertical_stiffness * x[c, at] * placed[s][2:3]
                    r[c, at] = r[c, at] - drop
            for ref, dst in ((x, inc_ref), (r, res_ref)):
                at = pl.ds(part * chunk, chunk)
                copy = pltpu.make_async_copy(
                    ref.at[c, at], dst.at[c, at], out_sem.at[len(stores)]
                )
                copy.start()
                stores.append(copy)
    for copy in stores:
        copy.wait()


def shards(right_side, mass_field, span_lengths, stick_flags, normal_load, prior_friction):
    sizes = (lax.axis_size("len"), lax.axis_size("xs"))
    rows = DEPTH * NS
    field = (3, rows, LANES)
    b = right_side.reshape(field)
    mass = mass_field.reshape(rows, LANES)
    spans = span_lengths.reshape(1, -1)
    stick = stick_flags.reshape(1, -1)
    load = normal_load.reshape(1, -1)
    anywhere = pl.BlockSpec(memory_space=pl.ANY)
    vmem = pl.BlockSpec(memory_space=pltpu.VMEM)
    v1, v2, v3, sums = pl.pallas_call(
        lambda *refs: krylov_kernel(sizes, *refs),
        name="krylov",
        out_shape=[jax.ShapeDtypeStruct(field, F32)] * 3
        + [jax.ShapeDtypeStruct((PARTIALS, LANES), F32)],
        in_specs=[anywhere, anywhere, vmem],
        out_specs=[vmem] * 4,
        scratch_shapes=[
            pltpu.VMEM((3, 3, PADDED, LANES), F32),
            pltpu.VMEM((rows, LANES), F32),
            pltpu.VMEM((PADDED, LANES), F32),
            pltpu.VMEM((4, 2, 3, STRIP_ROWS, LANES), F32),
            pltpu.VMEM((2, STRIP_ROWS, LANES), F32),
            pltpu.VMEM((2, STRIP_ROWS, LANES), F32),
            pltpu.VMEM((2, STRIP, LANES), F32),
            pltpu.VMEM((MESSAGE, LANES), F32),
            pltpu.VMEM((MESSAGE, LANES), F32),
            pltpu.VMEM((MESSAGE, LANES), F32),
            pltpu.VMEM((MESSAGE, LANES), F32),
            pltpu.VMEM((PARTIALS, LANES), F32),
            pltpu.VMEM((PARTIALS, LANES), F32),
            pltpu.VMEM((sizes[1], PARTIALS, LANES), F32),
            pltpu.VMEM((sizes[0], PARTIALS, LANES), F32),
            pltpu.SemaphoreType.DMA((4,)),
            pltpu.SemaphoreType.DMA((2,)),
            pltpu.SemaphoreType.DMA((2,)),
            pltpu.SemaphoreType.DMA((sizes[1],)),
            pltpu.SemaphoreType.DMA((sizes[1],)),
            pltpu.SemaphoreType.DMA((sizes[0],)),
            pltpu.SemaphoreType.DMA((sizes[0],)),
        ],
        compiler_params=pltpu.CompilerParams(collective_id=0, has_side_effects=True),
    )(b, mass, spans)
    increment, residual, friction = pl.pallas_call(
        finish_kernel,
        name="finish",
        out_shape=[
            jax.ShapeDtypeStruct(field, F32),
            jax.ShapeDtypeStruct(field, F32),
            jax.ShapeDtypeStruct(prior_friction.shape, F32),
        ],
        in_specs=[anywhere] + [vmem] * 8,
        out_specs=[anywhere, anywhere, vmem],
        scratch_shapes=[
            pltpu.VMEM(field, F32),
            pltpu.VMEM(field, F32),
            pltpu.VMEM(field, F32),
            pltpu.SemaphoreType.DMA((3,)),
            pltpu.SemaphoreType.DMA((12,)),
        ],
    )(b, v1, v2, v3, sums, spans, stick, load, prior_friction)
    return (
        increment.reshape(right_side.shape),
        residual.reshape(right_side.shape),
        friction,
    )


def solution(mesh):
    along = ("len", "xs")
    in_specs = (P(None, None, None, along), P(None, None, along), P(), P(), P(), P())
    out_specs = (P(None, None, None, along), P(None, None, None, along), P())
    return jax.shard_map(shards, mesh=mesh, in_specs=in_specs, out_specs=out_specs, check_vma=False)
```

time: 570 us -> 55.7 us (0.10); the launches traced: 561 us -> 55.3 us
  blocking collectives: 414 us -> 0 us
  other arithmetic: 63.3 us -> 0 us
  Pallas kernels: 0 us -> 54.7 us
  local copies, waits for them, and re-layouts: 36.9 us -> 0 us
  starting transfers between devices: 33.4 us -> 0 us
  between operations: 8.1 us -> 0.64 us
    psum x6 -> x0, blocking collectives: 414 us -> none  [the longest x2 147 us: shards(): curvature = lax.psum(jnp.sum(direction * image), ('len', 'xs'))]
    pallas_call x0 -> x2, Pallas kernels: none -> 54.7 us  [the longest x1 48.7 us: shards(): pl.pallas_call(lambda *refs: krylov_kernel(sizes, *refs), name='krylov',...]
    ppermute x12 -> x0, starting transfers between devices: 33.4 us -> none  [the longest x6 20.7 us: extended_2(): lax.ppermute(tail, axis, [(i, (i + 1) % count) for i in range(ends)])]
    add x11 -> x0, other arithmetic: 24 us -> none  [the longest x2 15.4 us: operate(): mass_field[None] * field + shear_modulus * laplacian]
    slice x10 -> x0, local copies, waits for them, and re-layouts: 17.2 us -> none  [the longest x8 13.4 us: extended_2(): lax.slice_in_dim(cells, cells.shape[dim] - width, cells.shape[dim], axis=...]
    concatenate x7 -> x0, other arithmetic: 16.2 us -> none  [the longest x6 16.2 us: extended_2(): jnp.concatenate([lax.ppermute(tail, axis, [(i, (i + 1) % count) for i in...]
    reduce_sum x6 -> x0, other arithmetic: 15.9 us -> none  [the longest x2 8.31 us: shards(): norm_next = lax.psum(jnp.sum(solved * solved), ('len', 'xs'))]
    ppermute x6 -> x0, local copies, waits for them, and re-layouts: 8.99 us -> none  [the longest x3 5.07 us: extended_2(): lax.ppermute(head, axis, [((i + 1) % count, i) for i in range(ends)])]
  transfers between devices with their start and end apart: 12 -> 0, of which waited for: 3 -> 0; matrix products, arithmetic and copies ran while one was open for 6% -> 0% of each run, Pallas kernels for 0% -> 0%
where the time goes in v1:
time: 55.7 us; the launch traced here: 55.3 us
  Pallas kernels  54.7 us (98%)
  between operations  0.64 us (1%)
    pallas_call x1, Pallas kernels, shards(): pl.pallas_call(lambda *refs: krylov_kernel(sizes, *refs), name='krylov',...  48.7 us
    pallas_call x1, Pallas kernels, shards(): pl.pallas_call(finish_kernel, name='finish', out_shape=[jax.ShapeDtypeStr...  5.94 us

profile of v1, /device:TPU:1, one launch (start us, length us, event | category | flops | bytes accessed | tf_op | source)
XLA Modules:
  0.0 55.3 jit_solution(1270998091203957777)
XLA Ops:
  0.6 48.7 %krylov.1 = (f32[3,1024,128]{2,1,0:T(8,128)}, f32[3,1024,128]{2,1,0:T(8,128)}, f32[3,1024,128]{2,1,0:T(8,128)}, f32[24,128]{1,0:T(8,128)}) custom-call(f32[3,1024,128]{2,1,0:T(8,128)} %bitcast.7, f32[1024,128]{1,0:T(8,128)} %bitcast.9, s32[1,128]{1,0:T(1,128)} %bitcast.10), custom_call_target="tpu_custom_call" | custom-call | tf_op jit(solution)/shard_map/krylov/pallas_call | solution.py:641
  49.4 5.9 %finish.1 = (f32[3,1024,128]{2,1,0:T(8,128)}, f32[3,1024,128]{2,1,0:T(8,128)}, f32[2,256]{1,0:T(2,128)}) custom-call(f32[3,1024,128]{2,1,0:T(8,128)} %bitcast.8, f32[3,1024,128]{2,1,0:T(8,128)} %get-tuple-element.10.v1_ref, f32[3,1024,128]{2,1,0:T(8,128)} %get-tuple-element.11.v2_ref, f32[3,1024,128]{2,1,0:T(8,128)} %get-tuple-element.12.v3_ref, ...), custom_call_target="tpu_custom_call" | custom-call | tf_op jit(solution)/shard_map/finish/pallas_call | solution.py:674

commit v2 on v1

v2 whole, which is shorter than its diff:
```python
import jax
import jax.numpy as jnp
from jax import lax
from jax.experimental import pallas as pl
from jax.experimental.pallas import tpu as pltpu
from jax.sharding import PartitionSpec as P

shear_modulus = 1.0
bulk_modulus = 1.5
elastic_stiffness = 8.0
pendulum_radius = 4.0
vertical_stiffness = 5.0
static_friction = 0.6
kinetic_friction = 0.45

DEPTH = 16
NS = 64
LANES = 128
PITCH = NS + 8
PADDED = (DEPTH + 3) * PITCH
HALO = 6
PAIRS = DEPTH * NS // LANES
WIDE = 3 * HALO
SECTION = 24
STRIP = WIDE * SECTION
OWN = 2 * HALO * 4 * PAIRS
LANDED = HALO * 4 * PAIRS

UNROLL = 2

MESH = pl.DeviceIdType.MESH
HIGHEST = lax.Precision.HIGHEST
F32 = jnp.float32


def two_sum(a, b):
    s = a + b
    t = s - a
    return s, (a - (s - t)) + (b - t)


def fold(block):
    return jnp.sum(block.reshape(block.shape[0] // 8, 8, LANES), axis=0)


def bearing_ends(spans):
    piers = spans.shape[1]
    upto = (
        lax.broadcasted_iota(jnp.int32, (piers, 2 * piers), 0)
        <= lax.broadcasted_iota(jnp.int32, (piers, 2 * piers), 1) // 2
    ).astype(F32)
    return (
        jnp.dot(
            jnp.broadcast_to(spans.astype(F32), (8, piers)),
            upto,
            precision=HIGHEST,
            preferred_element_type=F32,
        )[0:1]
        - 1.0
    )


def bearing_hits(ends, start):
    bearings = ends.shape[1]
    along = lax.broadcasted_iota(jnp.int32, (LANES, bearings), 0) + start
    side = lax.rem(lax.broadcasted_iota(jnp.int32, (LANES, bearings), 1), 2)
    here = along.astype(F32) == ends
    return [jnp.where(here & (side == s), 1.0, 0.0).astype(F32) for s in range(2)]


def krylov_kernel(
    sizes,
    b_ref,
    mass_ref,
    spans_ref,
    out1_ref,
    out2_ref,
    out3_ref,
    coefficients_ref,
    sites_ref,
    v0,
    v1,
    v2,
    mass,
    w,
    x0,
    x1,
    x2,
    x3,
    strip_mass,
    strip_w,
    near_left,
    near_right,
    valid,
    back,
    hit,
    part_a,
    part_b,
    slots_a,
    slots_b,
    site_a,
    site_b,
    site_slots_a,
    site_slots_b,
    in_sem,
    halo_send,
    halo_recv,
    a_send,
    a_recv,
    b_send,
    b_recv,
    site_a_send,
    site_a_recv,
    site_b_send,
    site_b_recv,
):
    len_size, xs_size = sizes
    count = len_size * xs_size
    at_len, at_xs = lax.axis_index("len"), lax.axis_index("xs")
    me = at_len * xs_size + at_xs
    left, right = lax.rem(me + count - 1, count), lax.rem(me + 1, count)
    place = lambda i: (i // xs_size, lax.rem(i, xs_size))
    group_a = [(at_len, lax.rem(at_xs + k, xs_size)) for k in range(1, xs_size)]
    group_b = [(lax.rem(at_len + k, len_size), at_xs) for k in range(1, len_size)]

    def load(d, carry):
        for c in range(3):
            pltpu.make_async_copy(
                b_ref.at[c, pl.ds(d * NS, NS)],
                v0.at[c, pl.ds((d + 1) * PITCH, NS)],
                in_sem.at[c],
            ).start()
        return carry

    lax.fori_loop(0, DEPTH, load, 0)
    pltpu.make_async_copy(mass_ref, mass, in_sem.at[3]).start()

    barrier = pltpu.get_barrier_semaphore()
    partners = [place(left), place(right)] + group_b + group_a
    for partner in partners:
        pl.semaphore_signal(barrier, inc=1, device_id=partner, device_id_type=MESH)

    for c in range(4):
        if c < 3:
            pltpu.make_async_copy(
                b_ref.at[c], v0.at[c, pl.ds(0, DEPTH * NS)], in_sem.at[c]
            ).wait()
        else:
            pltpu.make_async_copy(mass_ref, mass, in_sem.at[3]).wait()

        def edges(i, carry, c=c):
            for j in range(4):
                t = i * 4 + j
                if c < 3:
                    tile = jnp.concatenate(
                        [v0[c, pl.ds((2 * t + 1 + e) * PITCH, NS)] for e in range(2)], axis=0
                    )
                else:
                    tile = mass[pl.ds(t * LANES, LANES)]
                turned = tile.T
                at = c * PAIRS + t
                pitch = 4 * PAIRS
                near_left[pl.ds(LANDED + at, 8, stride=pitch), :] = turned[0:8]
                near_left[pl.ds(LANDED + 8 * pitch + at, 4, stride=pitch), :] = turned[8:12]
                near_right[pl.ds(at, 4, stride=pitch), :] = turned[LANES - 12 : LANES - 8]
                near_right[pl.ds(4 * pitch + at, 8, stride=pitch), :] = turned[LANES - 8 :]
            return carry

        lax.fori_loop(0, PAIRS // 4, edges, 0)

    pl.semaphore_wait(barrier, len(partners))
    middle = pl.ds(LANDED, LANDED)
    halos = [
        pltpu.make_async_remote_copy(
            src_ref=near_left.at[middle],
            dst_ref=near_right.at[pl.ds(2 * LANDED, LANDED)],
            send_sem=halo_send.at[0],
            recv_sem=halo_recv.at[0],
            device_id=place(left),
            device_id_type=MESH,
        ),
        pltpu.make_async_remote_copy(
            src_ref=near_right.at[middle],
            dst_ref=near_left.at[pl.ds(0, LANDED)],
            send_sem=halo_send.at[1],
            recv_sem=halo_recv.at[1],
            device_id=place(right),
            device_id_type=MESH,
        ),
    ]
    for copy in halos:
        copy.start()

    def guard(d, carry):
        row = (d + 1) * PITCH + NS
        for ref in (v0, v1, v2):
            for c in range(3):
                ref[c, pl.ds(row, 8)] = jnp.zeros((8, LANES), F32)
        w[pl.ds(row, 8)] = jnp.zeros((8, LANES), F32)
        return carry

    lax.fori_loop(0, DEPTH, guard, 0)
    for start in (0, (DEPTH + 1) * PITCH):
        for ref in (v0, v1, v2):
            for c in range(3):
                ref[c, pl.ds(start, PITCH)] = jnp.zeros((PITCH, LANES), F32)
        w[pl.ds(start, PITCH)] = jnp.zeros((PITCH, LANES), F32)
    for c in range(3):
        for ref in (v0, v1, v2):
            ref[c, pl.ds((DEPTH + 2) * PITCH, PITCH)] = jnp.zeros((PITCH, LANES), F32)

    has_left = jnp.where(me > 0, 1.0, 0.0).astype(F32)
    has_right = jnp.where(me < count - 1, 1.0, 0.0).astype(F32)
    low = lax.broadcasted_iota(jnp.int32, (8, LANES), 1) < LANES // 2

    def guard_strip(p, carry):
        row = p * SECTION + 8
        for ref in (x0, x1, x2):
            for c in range(3):
                ref[c, pl.ds(row, 8)] = jnp.zeros((8, LANES), F32)
        strip_w[pl.ds(row, 8)] = jnp.zeros((8, LANES), F32)
        valid[p] = jnp.where(
            low,
            jnp.where(p < HALO, has_left, 1.0),
            jnp.where(p >= 2 * HALO, has_right, 1.0),
        )
        return carry

    lax.fori_loop(0, WIDE, guard_strip, 0)

    def apply(source, target, last, dots):
        quarter = 0.25 * bulk_modulus

        def divergence(base, scale):
            first = source[0, pl.ds(base, NS)]
            along = pltpu.roll(first, LANES - 1, 1) - pltpu.roll(first, 1, 1)
            across = source[1, pl.ds(base + 1, NS)] - source[1, pl.ds(base - 1, NS)]
            depth = source[2, pl.ds(base + PITCH, NS)] - source[2, pl.ds(base - PITCH, NS)]
            return scale * (along + across + depth)

        w[pl.ds(PITCH, NS)] = divergence(PITCH, quarter)
        zero = jnp.zeros((8, LANES), F32)

        def body(d, sums):
            base = (d + 1) * PITCH
            heavy = mass[pl.ds(d * NS, NS)] + 6.0
            ahead = divergence(base + PITCH, jnp.where(d < DEPTH - 1, quarter, 0.0))
            local = w[pl.ds(base, NS)]
            beside = (
                w[pl.ds(base + 1, NS)] - w[pl.ds(base - 1, NS)],
                ahead - w[pl.ds(base - PITCH, NS)],
            )
            terms = [zero] * len(dots)
            for c in range(3):
                here = source[c, pl.ds(base, NS)]
                if c == 0:
                    swept = pltpu.roll(here + local, LANES - 1, 1) + pltpu.roll(
                        here - local, 1, 1
                    )
                else:
                    swept = (
                        pltpu.roll(here, LANES - 1, 1)
                        + pltpu.roll(here, 1, 1)
                        + beside[c - 1]
                    )
                image = heavy * here
                image = image - (
                    source[c, pl.ds(base + 1, NS)] + source[c, pl.ds(base - 1, NS)]
                )
                image = image - (
                    source[c, pl.ds(base + PITCH, NS)] + source[c, pl.ds(base - PITCH, NS)]
                )
                image = image - swept
                if last:
                    target[c, pl.ds(d * NS, NS)] = image
                else:
                    target[c, pl.ds(base, NS)] = image
                for n, kind in enumerate(dots):
                    terms[n] = terms[n] + fold(
                        {"vv": here * here, "vi": here * image, "ii": image * image}[kind]
                    )
            w[pl.ds(base + PITCH, NS)] = ahead
            return tuple(s + t for s, t in zip(sums, terms))

        return lax.fori_loop(0, DEPTH, body, (zero,) * len(dots), unroll=UNROLL)

    mu0, mu1, mu2 = apply(v0, v1, False, ("vv", "vi", "ii"))
    mu3, mu4 = apply(v1, v2, False, ("vi", "ii"))
    (mu5,) = apply(v2, out3_ref, True, ("vi",))
    lane = lax.broadcasted_iota(jnp.int32, (8, LANES), 1)
    inner = (lane >= HALO) & (lane < LANES - HALO)
    moments = tuple(jnp.where(inner, mu, 0.0) for mu in (mu0, mu1, mu2, mu3, mu4, mu5))
    hits = bearing_hits(bearing_ends(spans_ref[...]), me * LANES)
    for s in range(2):
        hit[s] = hits[s]

    half = LANES // 2
    for copy in halos:
        copy.wait_recv()

    def mix(first, second):
        turned = pltpu.roll(jnp.where(low, second, first), half, 1)
        return jnp.where(low, first, turned), jnp.where(low, turned, second)

    def gather(p, carry):
        for c in range(4):
            at = pl.ds(pl.multiple_of((p * 4 + c) * PAIRS, 8), PAIRS)
            even, odd = mix(near_left[at], near_right[at])
            for part, value in ((0, even), (16, odd)):
                to = pl.ds(pl.multiple_of(p * SECTION + part, 8), 8)
                if c < 3:
                    x0[c, to] = value * valid[p]
                else:
                    strip_mass[to] = value
        return carry

    lax.fori_loop(0, WIDE, gather, 0, unroll=6)

    across_at = lax.rem(lax.broadcasted_iota(jnp.int32, (8, LANES), 1), half)

    def after(x):
        return jnp.where(across_at == half - 1, 0.0, pltpu.roll(x, LANES - 1, 1))

    def before(x):
        return jnp.where(across_at == 0, 0.0, pltpu.roll(x, 1, 1))

    def rows(ref, row):
        return ref[pl.ds(row, 8)], ref[pl.ds(row + 16, 8)]

    def beside(ref, row, pair):
        even, odd = pair
        return (odd, ref[pl.ds(row + 15, 8)]), (ref[pl.ds(row + 1, 8)], even)

    zero = jnp.zeros((8, LANES), F32)
    sums = (zero,) * 6
    xs = (x0, x1, x2, x3)
    for k in range(3):
        source, target = xs[k], xs[k + 1]

        def strip_divergence(i, carry, k=k, source=source):
            p = i + 2 * k + 1
            row = p * SECTION
            first, second = rows(source.at[0], row - SECTION), rows(source.at[0], row + SECTION)
            middle = rows(source.at[1], row)
            third = beside(source.at[2], row, rows(source.at[2], row))
            for e in range(2):
                strip_w[pl.ds(row + 16 * e, 8)] = (
                    (0.25 * bulk_modulus)
                    * (
                        (second[e] - first[e])
                        + (after(middle[e]) - before(middle[e]))
                        + (third[e][0] - third[e][1])
                    )
                    * valid[p]
                )
            return carry

        lax.fori_loop(0, WIDE - 2 - 4 * k, strip_divergence, 0, unroll=4)

        def strip_image(i, sums, k=k, source=source, target=target):
            p = i + 2 * k + 2
            row = p * SECTION
            heavy = rows(strip_mass, row)
            local = rows(strip_w, row)
            around = rows(strip_w, row - SECTION), rows(strip_w, row + SECTION)
            upright = beside(strip_w, row, local)
            images, heres = [], []
            for c in range(3):
                ref = source.at[c]
                here = rows(ref, row)
                along = rows(ref, row - SECTION), rows(ref, row + SECTION)
                depth = beside(ref, row, here)
                for e in range(2):
                    image = (heavy[e] + 6.0) * here[e] - (along[0][e] + along[1][e])
                    image = image - (depth[e][0] + depth[e][1])
                    if c == 1:
                        image = image - (after(here[e] + local[e]) + before(here[e] - local[e]))
                    else:
                        image = image - (after(here[e]) + before(here[e]))
                    if c == 0:
                        image = image - (around[1][e] - around[0][e])
                    elif c == 2:
                        image = image - (upright[e][0] - upright[e][1])
                    images.append(image * valid[p])
                    heres.append(here[e])
            sums = list(sums)
            for n, (image, here) in enumerate(zip(images, heres)):
                at = pl.ds(row + 16 * (n % 2), 8)
                target[n // 2, at] = image
                if k == 2:
                    z0, z1 = x0[n // 2, at], x1[n // 2, at]
                    for m, (p0, p1) in enumerate(
                        ((z0, z0), (z0, z1), (z1, z1), (z1, here), (here, here), (here, image))
                    ):
                        sums[m] = sums[m] + p0 * p1
            return tuple(sums)

        sums = lax.fori_loop(0, WIDE - 4 - 4 * k, strip_image, sums, unroll=2)
    strips = sums

    def exchange(source, slots, partners, own, send_sems, recv_sems):
        copies = []
        for k, partner in enumerate(partners):
            copy = pltpu.make_async_remote_copy(
                src_ref=source,
                dst_ref=slots.at[own],
                send_sem=send_sems.at[k],
                recv_sem=recv_sems.at[k],
                device_id=partner,
                device_id_type=MESH,
            )
            copy.start()
            copies.append(copy)
        slots[own] = source[...]
        return copies

    def tree(parts, join):
        while len(parts) > 1:
            joined = [join(parts[i], parts[i + 1]) for i in range(0, len(parts) - 1, 2)]
            parts = joined + parts[len(parts) - len(parts) % 2 :]
        return parts[0]

    def join(p, q):
        hi, more = two_sum(p[0], q[0])
        return hi, p[1] + q[1] + more

    def total(slots, number):
        return tree([(slots[i, 0:8], slots[i, 8:16]) for i in range(number)], join)

    head, rest = [], []
    for n in range(6):
        hi, lo = two_sum(moments[n], strips[n])
        for shift in (4, 2, 1):
            hi, more = two_sum(hi, pltpu.roll(hi, shift, 0))
            lo = lo + pltpu.roll(lo, shift, 0) + more
        head.append(hi[0:1])
        rest.append(lo[0:1])
    blank = [jnp.zeros((2, LANES), F32)]
    part_a[...] = jnp.concatenate(head + blank + rest + blank, axis=0)
    copies = list(halos)
    copies_a = exchange(part_a, slots_a, group_a, at_xs, a_send, a_recv)

    edge_rows = 16 * PAIRS
    lanes = lax.broadcasted_iota(jnp.int32, (LANES, LANES), 1)
    outer = (lanes < HALO) | (lanes >= LANES - HALO)
    mains = (v1, v2, None)
    outs = (out1_ref, out2_ref, out3_ref)

    def back_edges(i, carry, ks=(0, 1, 2)):
        for k in ks:
            for c in range(3):
                even, odd = rows(xs[k + 1].at[c], (i + HALO) * SECTION)
                first, second = mix(even, odd)
                slot = (k * 3 + c) * edge_rows
                back[pl.ds(slot + (8 + i) * PAIRS, PAIRS)] = first
                back[pl.ds(slot + (2 + i) * PAIRS, PAIRS)] = second
        return carry

    def merge(k, c, t):
        slot = (k * 3 + c) * edge_rows + t
        edge = jnp.concatenate(
            [
                back[pl.ds(slot + 8 * PAIRS, 8, stride=PAIRS), :],
                jnp.zeros((LANES - 16, LANES), F32),
                back[pl.ds(slot, 8, stride=PAIRS), :],
            ],
            axis=0,
        ).T
        if k < 2:
            main = jnp.concatenate(
                [mains[k][c, pl.ds((2 * t + 1 + e) * PITCH, NS)] for e in range(2)], axis=0
            )
        else:
            main = out3_ref[c, pl.ds(t * LANES, LANES)]
        outs[k][c, pl.ds(t * LANES, LANES)] = jnp.where(outer, edge, main)

    for slot in range(9):
        for r in (0, 1, 14, 15):
            back[pl.ds(slot * edge_rows + r * PAIRS, PAIRS)] = jnp.zeros((PAIRS, LANES), F32)
    lax.fori_loop(0, HALO, back_edges, 0)
    for k in (0, 1):
        for c in (0, 1):
            merge(k, c, 0)

    site = jnp.zeros((8, 2 * LANES), F32)
    for s, across in ((0, NS // 4), (1, 3 * NS // 4)):
        picked = [v0[c, pl.ds(PITCH + across, 1)] for c in (0, 1)]
        picked += [out1_ref[c, pl.ds(across, 1)] for c in (0, 1)]
        picked += [out2_ref[c, pl.ds(across, 1)] for c in (0, 1)]
        picked += [jnp.zeros((2, LANES), F32)]
        site = site + jnp.dot(
            jnp.concatenate(picked, axis=0),
            hit[s],
            precision=HIGHEST,
            preferred_element_type=F32,
        )
    site_a[...] = jnp.concatenate([site[:, :LANES], site[:, LANES:]], axis=0)
    copies_sa = exchange(site_a, site_slots_a, group_a, at_xs, site_a_send, site_a_recv)

    for copy in copies_a:
        copy.wait_recv()
    part_b[...] = jnp.concatenate(total(slots_a, xs_size), axis=0)
    copies_b = exchange(part_b, slots_b, group_b, at_len, b_send, b_recv)

    for copy in copies_sa:
        copy.wait_recv()
    site_b[...] = tree([site_slots_a[i] for i in range(xs_size)], jnp.add)
    copies_sb = exchange(site_b, site_slots_b, group_b, at_len, site_b_send, site_b_recv)

    for k, c in ((0, 2), (1, 2), (2, 0), (2, 1), (2, 2)):
        merge(k, c, 0)

    def merge_rest(t, carry):
        for k in range(3):
            for c in range(3):
                merge(k, c, t)
        return carry

    lax.fori_loop(1, PAIRS, merge_rest, 0)

    for copy in copies_b:
        copy.wait_recv()
    increment, solved = steps(*total(slots_b, len_size))
    coefficients_ref[...] = jnp.concatenate(
        list(increment) + list(solved) + [jnp.zeros((1, LANES), F32)], axis=0
    )
    for copy in copies_sb:
        copy.wait_recv()
    sites_ref[...] = tree([site_slots_b[i] for i in range(len_size)], jnp.add)
    for copy in halos + copies_a + copies_b + copies_sa + copies_sb:
        copy.wait_send()


def steps(hi, lo):
    for shift in (64, 32, 16, 8, 4, 2, 1):
        hi, more = two_sum(hi, pltpu.roll(hi, shift, 1))
        lo = lo + pltpu.roll(lo, shift, 1) + more
    hi, lo = two_sum(hi, lo)
    theta = jnp.round(hi[1:2] / hi[0:1] * 64.0) * (1.0 / 64.0)
    central = [hi[0:1]]
    for order in range(5):
        n = 5 - order
        big = hi[:n] * 4097.0
        upper = big - (big - hi[:n])
        lower = hi[:n] - upper
        value, more = two_sum(hi[1 : n + 1], -theta * upper)
        value, extra = two_sum(value, -theta * lower)
        low_part = lo[1 : n + 1] - theta * lo[:n] + (more + extra)
        hi, lo = two_sum(value, low_part)
        central.append(hi[0:1])
    scale = 1.0 / central[0]
    c = [x * scale for x in central]
    c1 = [c[i + 1] + theta * c[i] for i in range(5)]

    def form(p, moments):
        terms = None
        for i in range(len(p)):
            for j in range(i, len(p)):
                term = (1.0 if i == j else 2.0) * (p[i] * p[j]) * moments[i + j]
                terms = term if terms is None else terms + term
        return terms

    one, zero = jnp.ones_like(theta), jnp.zeros_like(theta)
    left, ahead, norm = [one], [one], c[0]
    increment = [zero, zero, zero]
    for iteration in range(3):
        alpha = norm / form(ahead, c1)
        increment = [
            x + alpha * ahead[i] if i < len(ahead) else x for i, x in enumerate(increment)
        ]
        image = [theta * x for x in ahead] + [zero]
        image = [image[i] + (ahead[i - 1] if i else zero) for i in range(len(image))]
        left = left + [zero]
        left = [x - alpha * y for x, y in zip(left, image)]
        if iteration < 2:
            after = form(left, c)
            beta = after / norm
            ahead = ahead + [zero]
            ahead = [x + beta * y for x, y in zip(left, ahead)]
            norm = after
    x0, x1, x2 = increment
    r0, r1, r2, r3 = left
    increment = (x0 - theta * (x1 - theta * x2), x1 - 2.0 * theta * x2, x2)
    solved = (
        r0 - theta * (r1 - theta * (r2 - theta * r3)),
        r1 - theta * (2.0 * r2 - 3.0 * theta * r3),
        r2 - 3.0 * theta * r3,
        r3,
    )
    return increment, solved


def finish_kernel(
    b_ref,
    v1_ref,
    v2_ref,
    v3_ref,
    coefficients_ref,
    sites_ref,
    spans_ref,
    stick_ref,
    load_ref,
    prior_ref,
    inc_ref,
    res_ref,
    friction_ref,
    b,
    x,
    r,
    in_sem,
    out_sem,
):
    loads = [pltpu.make_async_copy(b_ref.at[c], b.at[c], in_sem.at[c]) for c in range(3)]
    for copy in loads:
        copy.start()
    me = lax.axis_index("len") * lax.axis_size("xs") + lax.axis_index("xs")
    row = lambda n: coefficients_ref[pl.ds(n, 1)]
    x0, x1, x2 = row(0), row(1), row(2)
    stores = []

    def combine(c, at):
        p0, p1, p2, p3 = b[c, at], v1_ref[c, at], v2_ref[c, at], v3_ref[c, at]
        x[c, at] = x0 * p0 + x1 * p1 + x2 * p2
        r[c, at] = row(3) * p0 + row(4) * p1 + row(5) * p2 + row(6) * p3

    def store(c, at):
        for ref, dst in ((x, inc_ref), (r, res_ref)):
            copy = pltpu.make_async_copy(ref.at[c, at], dst.at[c, at], out_sem.at[len(stores)])
            copy.start()
            stores.append(copy)

    rows = DEPTH * NS
    for c in range(3):
        loads[c].wait()
        for first, last in ((NS, rows // 2), (rows // 2, rows)):

            def body(i, carry, c=c, first=first):
                combine(c, pl.ds(pl.multiple_of(first + i * NS, NS), NS))
                return carry

            lax.fori_loop(0, (last - first) // NS, body, 0)
            store(c, pl.ds(first, last - first))

    wide = lambda a: jnp.concatenate([a, a], axis=1)
    site = jnp.concatenate([sites_ref[0:8], sites_ref[8:16]], axis=1)
    readout = wide(x0) * site[0:2] + wide(x1) * site[2:4] + wide(x2) * site[4:6]
    radius = jnp.where(stick_ref[...] == 1, static_friction, kinetic_friction) * load_ref[...]
    trial = prior_ref[...] + elastic_stiffness * readout
    magnitude = jnp.sqrt(trial[0:1] * trial[0:1] + trial[1:2] * trial[1:2])
    friction = trial * (radius / jnp.maximum(magnitude, radius))
    friction_ref[...] = friction
    force = friction + load_ref[...] / pendulum_radius * readout
    bearings = force.shape[1]
    forces = jnp.concatenate(
        [force, jnp.ones((1, bearings), F32), jnp.zeros((5, bearings), F32)], axis=0
    )
    hits = bearing_hits(bearing_ends(spans_ref[...]), me * LANES)
    placed = [
        lax.dot_general(
            forces,
            hit,
            (((1,), (1,)), ((), ())),
            precision=HIGHEST,
            preferred_element_type=F32,
        )
        for hit in hits
    ]
    for c in range(3):
        combine(c, pl.ds(0, NS))
        for s, across in ((0, NS // 4), (1, 3 * NS // 4)):
            at = pl.ds(across, 1)
            if c < 2:
                drop = placed[s][c : c + 1]
            else:
                drop = vertical_stiffness * x[c, at] * placed[s][2:3]
            r[c, at] = r[c, at] - drop
        store(c, pl.ds(0, NS))
    for copy in stores:
        copy.wait()


def shards(right_side, mass_field, span_lengths, stick_flags, normal_load, prior_friction):
    sizes = (lax.axis_size("len"), lax.axis_size("xs"))
    rows = DEPTH * NS
    field = (3, rows, LANES)
    b = right_side.reshape(field)
    mass = mass_field.reshape(rows, LANES)
    spans = span_lengths.reshape(1, -1)
    stick = stick_flags.reshape(1, -1)
    load = normal_load.reshape(1, -1)
    anywhere = pl.BlockSpec(memory_space=pl.ANY)
    vmem = pl.BlockSpec(memory_space=pltpu.VMEM)
    v1, v2, v3, coefficients, sites = pl.pallas_call(
        lambda *refs: krylov_kernel(sizes, *refs),
        name="krylov",
        out_shape=[pltpu.VMEM(field, F32)] * 3
        + [pltpu.VMEM((8, LANES), F32), pltpu.VMEM((16, LANES), F32)],
        in_specs=[anywhere, anywhere, vmem],
        out_specs=[vmem] * 5,
        scratch_shapes=[pltpu.VMEM((3, PADDED, LANES), F32)] * 3
        + [pltpu.VMEM((rows, LANES), F32), pltpu.VMEM((PADDED, LANES), F32)]
        + [pltpu.VMEM((3, STRIP, LANES), F32)] * 4
        + [pltpu.VMEM((STRIP, LANES), F32)] * 2
        + [pltpu.VMEM((OWN + LANDED, LANES), F32)] * 2
        + [
            pltpu.VMEM((WIDE, 8, LANES), F32),
            pltpu.VMEM((9 * 16 * PAIRS, LANES), F32),
            pltpu.VMEM((2, LANES, 2 * LANES), F32),
        ]
        + [pltpu.VMEM((16, LANES), F32)] * 2
        + [pltpu.VMEM((n, 16, LANES), F32) for n in (sizes[1], sizes[0])]
        + [pltpu.VMEM((16, LANES), F32)] * 2
        + [pltpu.VMEM((n, 16, LANES), F32) for n in (sizes[1], sizes[0])]
        + [
            pltpu.SemaphoreType.DMA((n,))
            for n in (4, 2, 2) + 2 * (sizes[1], sizes[1], sizes[0], sizes[0])
        ],
        compiler_params=pltpu.CompilerParams(
            collective_id=0, has_side_effects=True, vmem_limit_bytes=32 * 2**20
        ),
    )(b, mass, spans)
    increment, residual, friction = pl.pallas_call(
        finish_kernel,
        name="finish",
        out_shape=[
            jax.ShapeDtypeStruct(field, F32),
            jax.ShapeDtypeStruct(field, F32),
            jax.ShapeDtypeStruct(prior_friction.shape, F32),
        ],
        in_specs=[anywhere] + [vmem] * 9,
        out_specs=[anywhere, anywhere, vmem],
        scratch_shapes=[
            pltpu.VMEM(field, F32),
            pltpu.VMEM(field, F32),
            pltpu.VMEM(field, F32),
            pltpu.SemaphoreType.DMA((3,)),
            pltpu.SemaphoreType.DMA((18,)),
        ],
        compiler_params=pltpu.CompilerParams(vmem_limit_bytes=24 * 2**20),
    )(b, v1, v2, v3, coefficients, sites, spans, stick, load, prior_friction)
    return (
        increment.reshape(right_side.shape),
        residual.reshape(right_side.shape),
        friction,
    )


def solution(mesh):
    along = ("len", "xs")
    in_specs = (P(None, None, None, along), P(None, None, along), P(), P(), P(), P())
    out_specs = (P(None, None, None, along), P(None, None, None, along), P())
    return jax.shard_map(shards, mesh=mesh, in_specs=in_specs, out_specs=out_specs, check_vma=False)
```

time: 55.7 us -> 37.2 us (0.67)
  Pallas kernels: 54.7 us -> 33.2 us
  local copies, waits for them, and re-layouts: 0 us -> 3.13 us
    pallas_call x1, Pallas kernels: 48.7 us -> 30.2 us  [shards(): pl.pallas_call(lambda *refs: krylov_kernel(sizes, *refs), name='krylov',...]
    unnamed x0 -> x12, local copies, waits for them, and re-layouts: none -> 3.13 us
    pallas_call x1, Pallas kernels: 5.94 us -> 2.93 us  [shards(): pl.pallas_call(finish_kernel, name='finish', out_shape=[jax.ShapeDtypeStr...]
where the time goes in v2:
time: 37.2 us; the launch traced here: 37 us
  Pallas kernels  33.2 us (89%)
  local copies, waits for them, and re-layouts  3.13 us (8%)
  between operations  0.7 us (2%)
    pallas_call x1, Pallas kernels, shards(): pl.pallas_call(lambda *refs: krylov_kernel(sizes, *refs), name='krylov',...  30.2 us
    unnamed x12, local copies, waits for them, and re-layouts  3.13 us
    pallas_call x1, Pallas kernels, shards(): pl.pallas_call(finish_kernel, name='finish', out_shape=[jax.ShapeDtypeStr...  2.93 us

profile of v2, /device:TPU:1, one launch (start us, length us, event | category | flops | bytes accessed | tf_op | source)
XLA Modules:
  0.0 37.0 jit_solution(15436459991171048072)
XLA Ops:
  0.6 0.0 copy-start.2
  0.6 0.0 copy-start.5
  0.7 0.0 copy-start.4
  0.7 0.0 copy-start
  0.7 1.4 %copy-done = f32[3,16,64,128]{3,2,1,0:T(8,128)S(1)} copy-done((f32[3,16,64,128]{3,2,1,0:T(8,128)S(1)}, f32[3,16,64,128]{3,2,1,0:T(8,128)}, u32[]{:S(2)}) %copy-start) | copy-done | bytes 1572888
  2.1 0.0 copy-start.1
  2.1 1.0 %copy-done.1 = f32[16,64,128]{2,1,0:T(8,128)S(1)} copy-done((f32[16,64,128]{2,1,0:T(8,128)S(1)}, f32[16,64,128]{2,1,0:T(8,128)}, u32[]{:S(2)}) %copy-start.1) | copy-done | bytes 524312
  3.1 0.0 copy-start.3
  3.1 0.7 %copy-done.3 = s32[128]{0:T(128)S(1)} copy-done((s32[128]{0:T(128)S(1)}, s32[128]{0:T(128)}, u32[]{:S(2)}) %copy-start.3) | copy-done | bytes 536
  3.8 30.2 %krylov.1 = (f32[3,1024,128]{2,1,0:T(8,128)S(1)}, f32[3,1024,128]{2,1,0:T(8,128)S(1)}, f32[3,1024,128]{2,1,0:T(8,128)S(1)}, f32[8,128]{1,0:T(8,128)S(1)}, f32[16,128]{1,0:T(8,128)S(1)}) custom-call(f32[3,1024,128]{2,1,0:T(8,128)S(1)} %bitcast.7, f32[1024,128]{1,0:T(8,128)S(1)} %bitcast.9, s32[1,128]{1,0:T(1,128)S(1)} %bitcast.10), custom_call_target="tpu_custom_call" | custom-call | tf_op jit(solution)/shard_map/krylov/pallas_call | solution.py:693
  34.0 0.0 copy-done.2
  34.0 0.0 copy-done.5
  34.0 0.0 copy-done.4
  34.1 2.9 %finish.1 = (f32[3,1024,128]{2,1,0:T(8,128)}, f32[3,1024,128]{2,1,0:T(8,128)}, f32[2,256]{1,0:T(2,128)}) custom-call(f32[3,1024,128]{2,1,0:T(8,128)S(1)} %bitcast.8, f32[3,1024,128]{2,1,0:T(8,128)S(1)} %get-tuple-element.11.v1_ref, f32[3,1024,128]{2,1,0:T(8,128)S(1)} %get-tuple-element.12.v2_ref, f32[3,1024,128]{2,1,0:T(8,128)S(1)} %get-tuple-element.13.v3_ref, ...), custom_call_target="tpu_custom_call" | custom-call | tf_op jit(solution)/shard_map/finish/pallas_call | solution.py:722
Async XLA Ops:
  0.6 33.4 %copy-start.2 = (f32[2,256]{1,0:T(2,128)S(1)}, f32[2,256]{1,0:T(2,128)}, u32[]{:S(2)}) copy-start(f32[2,256]{1,0:T(2,128)} %prior_ref.1) | copy-start | bytes 6148
  0.6 33.4 %copy-start.5 = (f32[256]{0:T(256)S(1)}, f32[256]{0:T(256)}, u32[]{:S(2)}) copy-start(f32[256]{0:T(256)} %param.10) | copy-start | bytes 3076
  0.7 33.4 %copy-start.4 = (s32[256]{0:T(256)S(1)}, s32[256]{0:T(256)}, u32[]{:S(2)}) copy-start(s32[256]{0:T(256)} %param.9) | copy-start | bytes 3076
  0.7 1.4 %copy-start = (f32[3,16,64,128]{3,2,1,0:T(8,128)S(1)}, f32[3,16,64,128]{3,2,1,0:T(8,128)}, u32[]{:S(2)}) copy-start(f32[3,16,64,128]{3,2,1,0:T(8,128)} %param.6) | copy-start | bytes 4718596
  2.1 1.0 %copy-start.1 = (f32[16,64,128]{2,1,0:T(8,128)S(1)}, f32[16,64,128]{2,1,0:T(8,128)}, u32[]{:S(2)}) copy-start(f32[16,64,128]{2,1,0:T(8,128)} %param.7) | copy-start | bytes 1572868
  3.1 0.7 %copy-start.3 = (s32[128]{0:T(128)S(1)}, s32[128]{0:T(128)}, u32[]{:S(2)}) copy-start(s32[128]{0:T(128)} %param.8) | copy-start | bytes 1540

commit v3 on v2

--- a/solution.py
+++ b/solution.py
@@ -73,6 +73,7 @@
     b_ref,
     mass_ref,
     spans_ref,
+    out0_ref,
     out1_ref,
     out2_ref,
     out3_ref,
@@ -94,6 +95,7 @@
     valid,
     back,
     hit,
+    spans,
     part_a,
     part_b,
     slots_a,
@@ -134,6 +136,9 @@
 
     lax.fori_loop(0, DEPTH, load, 0)
     pltpu.make_async_copy(mass_ref, mass, in_sem.at[3]).start()
+    spans_copy = pltpu.make_async_copy(spans_ref, spans, in_sem.at[4])
+    spans_copy.start()
+    whole_copy = pltpu.make_async_copy(b_ref, out0_ref, in_sem.at[5])
 
     barrier = pltpu.get_barrier_semaphore()
     partners = [place(left), place(right)] + group_b + group_a
@@ -190,6 +195,8 @@
     ]
     for copy in halos:
         copy.start()
+
+    whole_copy.start()
 
     def guard(d, carry):
         row = (d + 1) * PITCH + NS
@@ -290,7 +297,9 @@
     lane = lax.broadcasted_iota(jnp.int32, (8, LANES), 1)
     inner = (lane >= HALO) & (lane < LANES - HALO)
     moments = tuple(jnp.where(inner, mu, 0.0) for mu in (mu0, mu1, mu2, mu3, mu4, mu5))
-    hits = bearing_hits(bearing_ends(spans_ref[...]), me * LANES)
+    spans_copy.wait()
+    whole_copy.wait()
+    hits = bearing_hits(bearing_ends(spans[...]), me * LANES)
     for s in range(2):
         hit[s] = hits[s]
 
@@ -604,22 +613,17 @@
     inc_ref,
     res_ref,
     friction_ref,
-    b,
     x,
     r,
-    in_sem,
     out_sem,
 ):
-    loads = [pltpu.make_async_copy(b_ref.at[c], b.at[c], in_sem.at[c]) for c in range(3)]
-    for copy in loads:
-        copy.start()
     me = lax.axis_index("len") * lax.axis_size("xs") + lax.axis_index("xs")
     row = lambda n: coefficients_ref[pl.ds(n, 1)]
     x0, x1, x2 = row(0), row(1), row(2)
     stores = []
 
     def combine(c, at):
-        p0, p1, p2, p3 = b[c, at], v1_ref[c, at], v2_ref[c, at], v3_ref[c, at]
+        p0, p1, p2, p3 = b_ref[c, at], v1_ref[c, at], v2_ref[c, at], v3_ref[c, at]
         x[c, at] = x0 * p0 + x1 * p1 + x2 * p2
         r[c, at] = row(3) * p0 + row(4) * p1 + row(5) * p2 + row(6) * p3
 
@@ -631,7 +635,6 @@
 
     rows = DEPTH * NS
     for c in range(3):
-        loads[c].wait()
         for first, last in ((NS, rows // 2), (rows // 2, rows)):
 
             def body(i, carry, c=c, first=first):
@@ -689,14 +692,16 @@
     stick = stick_flags.reshape(1, -1)
     load = normal_load.reshape(1, -1)
     anywhere = pl.BlockSpec(memory_space=pl.ANY)
+    hbm = pl.BlockSpec(memory_space=pltpu.HBM)
+    far = lambda a: pltpu.with_memory_space_constraint(a, pltpu.HBM)
     vmem = pl.BlockSpec(memory_space=pltpu.VMEM)
-    v1, v2, v3, coefficients, sites = pl.pallas_call(
+    v0, v1, v2, v3, coefficients, sites = pl.pallas_call(
         lambda *refs: krylov_kernel(sizes, *refs),
         name="krylov",
-        out_shape=[pltpu.VMEM(field, F32)] * 3
+        out_shape=[pltpu.VMEM(field, F32)] * 4
         + [pltpu.VMEM((8, LANES), F32), pltpu.VMEM((16, LANES), F32)],
-        in_specs=[anywhere, anywhere, vmem],
-        out_specs=[vmem] * 5,
+        in_specs=[hbm] * 3,
+        out_specs=[vmem] * 6,
         scratch_shapes=[pltpu.VMEM((3, PADDED, LANES), F32)] * 3
         + [pltpu.VMEM((rows, LANES), F32), pltpu.VMEM((PADDED, LANES), F32)]
         + [pltpu.VMEM((3, STRIP, LANES), F32)] * 4
@@ -706,6 +711,7 @@
             pltpu.VMEM((WIDE, 8, LANES), F32),
             pltpu.VMEM((9 * 16 * PAIRS, LANES), F32),
             pltpu.VMEM((2, LANES, 2 * LANES), F32),
+            pltpu.VMEM(spans.shape, jnp.int32),
         ]
         + [pltpu.VMEM((16, LANES), F32)] * 2
         + [pltpu.VMEM((n, 16, LANES), F32) for n in (sizes[1], sizes[0])]
@@ -713,12 +719,12 @@
         + [pltpu.VMEM((n, 16, LANES), F32) for n in (sizes[1], sizes[0])]
         + [
             pltpu.SemaphoreType.DMA((n,))
-            for n in (4, 2, 2) + 2 * (sizes[1], sizes[1], sizes[0], sizes[0])
+            for n in (6, 2, 2) + 2 * (sizes[1], sizes[1], sizes[0], sizes[0])
         ],
         compiler_params=pltpu.CompilerParams(
             collective_id=0, has_side_effects=True, vmem_limit_bytes=32 * 2**20
         ),
-    )(b, mass, spans)
+    )(far(b), far(mass), far(spans))
     increment, residual, friction = pl.pallas_call(
         finish_kernel,
         name="finish",
@@ -727,17 +733,15 @@
             jax.ShapeDtypeStruct(field, F32),
             jax.ShapeDtypeStruct(prior_friction.shape, F32),
         ],
-        in_specs=[anywhere] + [vmem] * 9,
+        in_specs=[vmem] * 10,
         out_specs=[anywhere, anywhere, vmem],
         scratch_shapes=[
             pltpu.VMEM(field, F32),
             pltpu.VMEM(field, F32),
-            pltpu.VMEM(field, F32),
-            pltpu.SemaphoreType.DMA((3,)),
             pltpu.SemaphoreType.DMA((18,)),
         ],
         compiler_params=pltpu.CompilerParams(vmem_limit_bytes=24 * 2**20),
-    )(b, v1, v2, v3, coefficients, sites, spans, stick, load, prior_friction)
+    )(v0, v1, v2, v3, coefficients, sites, spans, stick, load, prior_friction)
     return (
         increment.reshape(right_side.shape),
         residual.reshape(right_side.shape),

time: 37.2 us -> 32 us (0.86)
  local copies, waits for them, and re-layouts: 3.13 us -> 0.02 us
  Pallas kernels: 33.2 us -> 31.2 us
    unnamed x12 -> x8, local copies, waits for them, and re-layouts: 3.13 us -> 0.02 us
    pallas_call x1, Pallas kernels: 30.2 us -> 28.4 us  [shards(): pl.pallas_call(lambda *refs: krylov_kernel(sizes, *refs), name='krylov',...]
where the time goes in v3:
time: 32 us; the launch traced here: 31.9 us
  Pallas kernels  31.2 us (98%)
  between operations  0.7 us (2%)
    pallas_call x1, Pallas kernels, shards(): pl.pallas_call(lambda *refs: krylov_kernel(sizes, *refs), name='krylov',...  28.4 us
    pallas_call x1, Pallas kernels, shards(): pl.pallas_call(finish_kernel, name='finish', out_shape=[jax.ShapeDtypeStr...  2.79 us

profile of v3, /device:TPU:1, one launch (start us, length us, event | category | flops | bytes accessed | tf_op | source)
XLA Modules:
  0.0 31.9 jit_solution(13066858582372995857)
XLA Ops:
  0.6 0.0 copy-start
  0.6 0.0 copy-start.3
  0.7 0.0 copy-start.2
  0.7 0.0 copy-start.1
  0.7 28.4 %krylov.1 = (f32[3,1024,128]{2,1,0:T(8,128)S(1)}, f32[3,1024,128]{2,1,0:T(8,128)S(1)}, f32[3,1024,128]{2,1,0:T(8,128)S(1)}, f32[3,1024,128]{2,1,0:T(8,128)S(1)},...) custom-call(f32[3,1024,128]{2,1,0:T(8,128)} %bitcast.11, f32[1024,128]{1,0:T(8,128)} %bitcast.12, s32[1,128]{1,0:T(1,128)} %bitcast.7), custom_call_target="tpu_custom_call" | custom-call | tf_op jit(solution)/shard_map/krylov/pallas_call | solution.py:698
  29.1 0.0 copy-done
  29.1 0.0 copy-done.3
  29.1 0.0 copy-done.2
  29.1 0.0 copy-done.1
  29.1 2.8 %finish.1 = (f32[3,1024,128]{2,1,0:T(8,128)}, f32[3,1024,128]{2,1,0:T(8,128)}, f32[2,256]{1,0:T(2,128)}) custom-call(f32[3,1024,128]{2,1,0:T(8,128)S(1)} %get-tuple-element.12.b_ref, f32[3,1024,128]{2,1,0:T(8,128)S(1)} %get-tuple-element.13.v1_ref, f32[3,1024,128]{2,1,0:T(8,128)S(1)} %get-tuple-element.14.v2_ref, ...), custom_call_target="tpu_custom_call" | custom-call | tf_op jit(solution)/shard_map/finish/pallas_call | solution.py:728
Async XLA Ops:
  0.6 28.4 %copy-start = (f32[2,256]{1,0:T(2,128)S(1)}, f32[2,256]{1,0:T(2,128)}, u32[]{:S(2)}) copy-start(f32[2,256]{1,0:T(2,128)} %prior_ref.1) | copy-start | bytes 6148
  0.6 28.4 %copy-start.3 = (f32[256]{0:T(256)S(1)}, f32[256]{0:T(256)}, u32[]{:S(2)}) copy-start(f32[256]{0:T(256)} %param.10) | copy-start | bytes 3076
  0.7 28.4 %copy-start.2 = (s32[256]{0:T(256)S(1)}, s32[256]{0:T(256)}, u32[]{:S(2)}) copy-start(s32[256]{0:T(256)} %param.9) | copy-start | bytes 3076
  0.7 28.4 %copy-start.1 = (s32[128]{0:T(128)S(1)}, s32[128]{0:T(128)}, u32[]{:S(2)}) copy-start(s32[128]{0:T(128)} %param.8) | copy-start | bytes 1540

commit v4 on v3

--- a/solution.py
+++ b/solution.py
@@ -26,7 +26,9 @@
 OWN = 2 * HALO * 4 * PAIRS
 LANDED = HALO * 4 * PAIRS
 
-UNROLL = 2
+UNROLL = 4
+DIV_UNROLL = (16, 12, 8)
+IMG_UNROLL = (7, 5, 6)
 
 MESH = pl.DeviceIdType.MESH
 HIGHEST = lax.Precision.HIGHEST
@@ -125,6 +127,8 @@
     group_a = [(at_len, lax.rem(at_xs + k, xs_size)) for k in range(1, xs_size)]
     group_b = [(lax.rem(at_len + k, len_size), at_xs) for k in range(1, len_size)]
 
+    spans_copy = pltpu.make_async_copy(spans_ref, spans, in_sem.at[4])
+    spans_copy.start()
     def load(d, carry):
         for c in range(3):
             pltpu.make_async_copy(
@@ -136,14 +140,54 @@
 
     lax.fori_loop(0, DEPTH, load, 0)
     pltpu.make_async_copy(mass_ref, mass, in_sem.at[3]).start()
-    spans_copy = pltpu.make_async_copy(spans_ref, spans, in_sem.at[4])
-    spans_copy.start()
     whole_copy = pltpu.make_async_copy(b_ref, out0_ref, in_sem.at[5])
 
     barrier = pltpu.get_barrier_semaphore()
     partners = [place(left), place(right)] + group_b + group_a
     for partner in partners:
         pl.semaphore_signal(barrier, inc=1, device_id=partner, device_id_type=MESH)
+
+    def guard(d, carry):
+        row = (d + 1) * PITCH + NS
+        for ref in (v0, v1, v2):
+            for c in range(3):
+                ref[c, pl.ds(row, 8)] = jnp.zeros((8, LANES), F32)
+        w[pl.ds(row, 8)] = jnp.zeros((8, LANES), F32)
+        return carry
+
+    lax.fori_loop(0, DEPTH, guard, 0)
+    for start in (0, (DEPTH + 1) * PITCH):
+        for ref in (v0, v1, v2):
+            for c in range(3):
+                ref[c, pl.ds(start, PITCH)] = jnp.zeros((PITCH, LANES), F32)
+        w[pl.ds(start, PITCH)] = jnp.zeros((PITCH, LANES), F32)
+    for c in range(3):
+        for ref in (v0, v1, v2):
+            ref[c, pl.ds((DEPTH + 2) * PITCH, PITCH)] = jnp.zeros((PITCH, LANES), F32)
+
+    has_left = jnp.where(me > 0, 1.0, 0.0).astype(F32)
+    has_right = jnp.where(me < count - 1, 1.0, 0.0).astype(F32)
+    low = lax.broadcasted_iota(jnp.int32, (8, LANES), 1) < LANES // 2
+
+    def guard_strip(p, carry):
+        row = p * SECTION + 8
+        for ref in (x0, x1, x2):
+            for c in range(3):
+                ref[c, pl.ds(row, 8)] = jnp.zeros((8, LANES), F32)
+        strip_w[pl.ds(row, 8)] = jnp.zeros((8, LANES), F32)
+        valid[p] = jnp.where(
+            low,
+            jnp.where(p < HALO, has_left, 1.0),
+            jnp.where(p >= 2 * HALO, has_right, 1.0),
+        )
+        return carry
+
+    lax.fori_loop(0, WIDE, guard_strip, 0)
+
+    spans_copy.wait()
+    hits = bearing_hits(bearing_ends(spans[...]), me * LANES)
+    for s in range(2):
+        hit[s] = hits[s]
 
     for c in range(4):
         if c < 3:
@@ -197,43 +241,6 @@
         copy.start()
 
     whole_copy.start()
-
-    def guard(d, carry):
-        row = (d + 1) * PITCH + NS
-        for ref in (v0, v1, v2):
-            for c in range(3):
-                ref[c, pl.ds(row, 8)] = jnp.zeros((8, LANES), F32)
-        w[pl.ds(row, 8)] = jnp.zeros((8, LANES), F32)
-        return carry
-
-    lax.fori_loop(0, DEPTH, guard, 0)
-    for start in (0, (DEPTH + 1) * PITCH):
-        for ref in (v0, v1, v2):
-            for c in range(3):
-                ref[c, pl.ds(start, PITCH)] = jnp.zeros((PITCH, LANES), F32)
-        w[pl.ds(start, PITCH)] = jnp.zeros((PITCH, LANES), F32)
-    for c in range(3):
-        for ref in (v0, v1, v2):
-            ref[c, pl.ds((DEPTH + 2) * PITCH, PITCH)] = jnp.zeros((PITCH, LANES), F32)
-
-    has_left = jnp.where(me > 0, 1.0, 0.0).astype(F32)
-    has_right = jnp.where(me < count - 1, 1.0, 0.0).astype(F32)
-    low = lax.broadcasted_iota(jnp.int32, (8, LANES), 1) < LANES // 2
-
-    def guard_strip(p, carry):
-        row = p * SECTION + 8
-        for ref in (x0, x1, x2):
-            for c in range(3):
-                ref[c, pl.ds(row, 8)] = jnp.zeros((8, LANES), F32)
-        strip_w[pl.ds(row, 8)] = jnp.zeros((8, LANES), F32)
-        valid[p] = jnp.where(
-            low,
-            jnp.where(p < HALO, has_left, 1.0),
-            jnp.where(p >= 2 * HALO, has_right, 1.0),
-        )
-        return carry
-
-    lax.fori_loop(0, WIDE, guard_strip, 0)
 
     def apply(source, target, last, dots):
         quarter = 0.25 * bulk_modulus
@@ -297,11 +304,7 @@
     lane = lax.broadcasted_iota(jnp.int32, (8, LANES), 1)
     inner = (lane >= HALO) & (lane < LANES - HALO)
     moments = tuple(jnp.where(inner, mu, 0.0) for mu in (mu0, mu1, mu2, mu3, mu4, mu5))
-    spans_copy.wait()
     whole_copy.wait()
-    hits = bearing_hits(bearing_ends(spans[...]), me * LANES)
-    for s in range(2):
-        hit[s] = hits[s]
 
     half = LANES // 2
     for copy in halos:
@@ -364,7 +367,7 @@
                 )
             return carry
 
-        lax.fori_loop(0, WIDE - 2 - 4 * k, strip_divergence, 0, unroll=4)
+        lax.fori_loop(0, WIDE - 2 - 4 * k, strip_divergence, 0, unroll=DIV_UNROLL[k])
 
         def strip_image(i, sums, k=k, source=source, target=target):
             p = i + 2 * k + 2
@@ -404,7 +407,7 @@
                         sums[m] = sums[m] + p0 * p1
             return tuple(sums)
 
-        sums = lax.fori_loop(0, WIDE - 4 - 4 * k, strip_image, sums, unroll=2)
+        sums = lax.fori_loop(0, WIDE - 4 - 4 * k, strip_image, sums, unroll=IMG_UNROLL[k])
     strips = sums
 
     def exchange(source, slots, partners, own, send_sems, recv_sems):
@@ -486,7 +489,7 @@
     for slot in range(9):
         for r in (0, 1, 14, 15):
             back[pl.ds(slot * edge_rows + r * PAIRS, PAIRS)] = jnp.zeros((PAIRS, LANES), F32)
-    lax.fori_loop(0, HALO, back_edges, 0)
+    lax.fori_loop(0, HALO, back_edges, 0, unroll=HALO)
     for k in (0, 1):
         for c in (0, 1):
             merge(k, c, 0)

time: 32 us -> 29.2 us (0.912)
  Pallas kernels: 31.2 us -> 28.3 us
    pallas_call x1, Pallas kernels: 28.4 us -> 25.5 us  [shards(): pl.pallas_call(lambda *refs: krylov_kernel(sizes, *refs), name='krylov',...]
where the time goes in v4:
time: 29.2 us; the launch traced here: 29.1 us
  Pallas kernels  28.3 us (97%)
  between operations  0.7 us (2%)
    pallas_call x1, Pallas kernels, shards(): pl.pallas_call(lambda *refs: krylov_kernel(sizes, *refs), name='krylov',...  25.5 us
    pallas_call x1, Pallas kernels, shards(): pl.pallas_call(finish_kernel, name='finish', out_shape=[jax.ShapeDtypeStr...  2.79 us

profile of v4, /device:TPU:1, one launch (start us, length us, event | category | flops | bytes accessed | tf_op | source)
XLA Modules:
  0.0 29.1 jit_solution(5969517573002300454)
XLA Ops:
  0.6 0.0 copy-start
  0.6 0.0 copy-start.3
  0.7 0.0 copy-start.2
  0.7 0.0 copy-start.1
  0.7 25.5 %krylov.1 = (f32[3,1024,128]{2,1,0:T(8,128)S(1)}, f32[3,1024,128]{2,1,0:T(8,128)S(1)}, f32[3,1024,128]{2,1,0:T(8,128)S(1)}, f32[3,1024,128]{2,1,0:T(8,128)S(1)},...) custom-call(f32[3,1024,128]{2,1,0:T(8,128)} %bitcast.11, f32[1024,128]{1,0:T(8,128)} %bitcast.12, s32[1,128]{1,0:T(1,128)} %bitcast.7), custom_call_target="tpu_custom_call" | custom-call | tf_op jit(solution)/shard_map/krylov/pallas_call | solution.py:701
  26.2 0.0 copy-done
  26.2 0.0 copy-done.3
  26.2 0.0 copy-done.2
  26.3 0.0 copy-done.1
  26.3 2.8 %finish.1 = (f32[3,1024,128]{2,1,0:T(8,128)}, f32[3,1024,128]{2,1,0:T(8,128)}, f32[2,256]{1,0:T(2,128)}) custom-call(f32[3,1024,128]{2,1,0:T(8,128)S(1)} %get-tuple-element.12.b_ref, f32[3,1024,128]{2,1,0:T(8,128)S(1)} %get-tuple-element.13.v1_ref, f32[3,1024,128]{2,1,0:T(8,128)S(1)} %get-tuple-element.14.v2_ref, ...), custom_call_target="tpu_custom_call" | custom-call | tf_op jit(solution)/shard_map/finish/pallas_call | solution.py:731
Async XLA Ops:
  0.6 25.6 %copy-start = (f32[2,256]{1,0:T(2,128)S(1)}, f32[2,256]{1,0:T(2,128)}, u32[]{:S(2)}) copy-start(f32[2,256]{1,0:T(2,128)} %prior_ref.1) | copy-start | bytes 6148
  0.6 25.6 %copy-start.3 = (f32[256]{0:T(256)S(1)}, f32[256]{0:T(256)}, u32[]{:S(2)}) copy-start(f32[256]{0:T(256)} %param.10) | copy-start | bytes 3076
  0.7 25.6 %copy-start.2 = (s32[256]{0:T(256)S(1)}, s32[256]{0:T(256)}, u32[]{:S(2)}) copy-start(s32[256]{0:T(256)} %param.9) | copy-start | bytes 3076
  0.7 25.6 %copy-start.1 = (s32[128]{0:T(128)S(1)}, s32[128]{0:T(128)}, u32[]{:S(2)}) copy-start(s32[128]{0:T(128)} %param.8) | copy-start | bytes 1540

commit v5 on v4

--- a/solution.py
+++ b/solution.py
@@ -75,15 +75,16 @@
     b_ref,
     mass_ref,
     spans_ref,
-    out0_ref,
-    out1_ref,
-    out2_ref,
-    out3_ref,
+    inc_ref,
+    solved_ref,
     coefficients_ref,
     sites_ref,
     v0,
     v1,
     v2,
+    out1_ref,
+    out2_ref,
+    out3_ref,
     mass,
     w,
     x0,
@@ -98,10 +99,8 @@
     back,
     hit,
     spans,
-    part_a,
-    part_b,
-    slots_a,
-    slots_b,
+    part,
+    slots,
     site_a,
     site_b,
     site_slots_a,
@@ -109,10 +108,9 @@
     in_sem,
     halo_send,
     halo_recv,
-    a_send,
-    a_recv,
-    b_send,
-    b_recv,
+    all_send,
+    all_recv,
+    ready,
     site_a_send,
     site_a_recv,
     site_b_send,
@@ -129,18 +127,18 @@
 
     spans_copy = pltpu.make_async_copy(spans_ref, spans, in_sem.at[4])
     spans_copy.start()
-    def load(d, carry):
-        for c in range(3):
+    for c in range(3):
+
+        def load(d, carry, c=c):
             pltpu.make_async_copy(
                 b_ref.at[c, pl.ds(d * NS, NS)],
                 v0.at[c, pl.ds((d + 1) * PITCH, NS)],
                 in_sem.at[c],
             ).start()
-        return carry
-
-    lax.fori_loop(0, DEPTH, load, 0)
+            return carry
+
+        lax.fori_loop(0, DEPTH, load, 0)
     pltpu.make_async_copy(mass_ref, mass, in_sem.at[3]).start()
-    whole_copy = pltpu.make_async_copy(b_ref, out0_ref, in_sem.at[5])
 
     barrier = pltpu.get_barrier_semaphore()
     partners = [place(left), place(right)] + group_b + group_a
@@ -239,8 +237,9 @@
     ]
     for copy in halos:
         copy.start()
-
-    whole_copy.start()
+    for partner in group_a:
+        pl.semaphore_signal(ready, inc=1, device_id=partner, device_id_type=MESH)
+
 
     def apply(source, target, last, dots):
         quarter = 0.25 * bulk_modulus
@@ -304,7 +303,6 @@
     lane = lax.broadcasted_iota(jnp.int32, (8, LANES), 1)
     inner = (lane >= HALO) & (lane < LANES - HALO)
     moments = tuple(jnp.where(inner, mu, 0.0) for mu in (mu0, mu1, mu2, mu3, mu4, mu5))
-    whole_copy.wait()
 
     half = LANES // 2
     for copy in halos:
@@ -343,10 +341,93 @@
         even, odd = pair
         return (odd, ref[pl.ds(row + 15, 8)]), (ref[pl.ds(row + 1, 8)], even)
 
+    xs = (x0, x1, x2, x3)
+    def exchange(source, slots, partners, own, send_sems, recv_sems):
+        copies = []
+        for k, partner in enumerate(partners):
+            copy = pltpu.make_async_remote_copy(
+                src_ref=source,
+                dst_ref=slots.at[own],
+                send_sem=send_sems.at[k],
+                recv_sem=recv_sems.at[k],
+                device_id=partner,
+                device_id_type=MESH,
+            )
+            copy.start()
+            copies.append(copy)
+        slots[own] = source[...]
+        return copies
+
+    def tree(parts, join):
+        while len(parts) > 1:
+            joined = [join(parts[i], parts[i + 1]) for i in range(0, len(parts) - 1, 2)]
+            parts = joined + parts[len(parts) - len(parts) % 2 :]
+        return parts[0]
+
+    def join(p, q):
+        hi, more = two_sum(p[0], q[0])
+        return hi, p[1] + q[1] + more
+
+    edge_rows = 16 * PAIRS
+    lanes = lax.broadcasted_iota(jnp.int32, (LANES, LANES), 1)
+    outer = (lanes < HALO) | (lanes >= LANES - HALO)
+    mains = (v1, v2, None)
+    outs = (out1_ref, out2_ref, out3_ref)
+
+    def back_edges(i, carry, ks=(0, 1, 2)):
+        for k in ks:
+            for c in range(3):
+                even, odd = rows(xs[k + 1].at[c], (i + HALO) * SECTION)
+                first, second = mix(even, odd)
+                slot = (k * 3 + c) * edge_rows
+                back[pl.ds(slot + (8 + i) * PAIRS, PAIRS)] = first
+                back[pl.ds(slot + (2 + i) * PAIRS, PAIRS)] = second
+        return carry
+
+    def merge(k, c, t):
+        slot = (k * 3 + c) * edge_rows + t
+        edge = jnp.concatenate(
+            [
+                back[pl.ds(slot + 8 * PAIRS, 8, stride=PAIRS), :],
+                jnp.zeros((LANES - 16, LANES), F32),
+                back[pl.ds(slot, 8, stride=PAIRS), :],
+            ],
+            axis=0,
+        ).T
+        if k < 2:
+            main = jnp.concatenate(
+                [mains[k][c, pl.ds((2 * t + 1 + e) * PITCH, NS)] for e in range(2)], axis=0
+            )
+        else:
+            main = out3_ref[c, pl.ds(t * LANES, LANES)]
+        outs[k][c, pl.ds(t * LANES, LANES)] = jnp.where(outer, edge, main)
+
     zero = jnp.zeros((8, LANES), F32)
     sums = (zero,) * 6
-    xs = (x0, x1, x2, x3)
     for k in range(3):
+        if k == 2:
+            for slot in range(9):
+                for r in (0, 1, 14, 15):
+                    back[pl.ds(slot * edge_rows + r * PAIRS, PAIRS)] = jnp.zeros((PAIRS, LANES), F32)
+            for i in range(HALO):
+                back_edges(i, 0, (0, 1))
+            for n in (0, 1):
+                for c in (0, 1):
+                    merge(n, c, 0)
+
+            site = jnp.zeros((8, 2 * LANES), F32)
+            for s, across in ((0, NS // 4), (1, 3 * NS // 4)):
+                picked = [v0[c, pl.ds(PITCH + across, 1)] for c in (0, 1)]
+                picked += [out1_ref[c, pl.ds(across, 1)] for c in (0, 1)]
+                picked += [out2_ref[c, pl.ds(across, 1)] for c in (0, 1)]
+                picked += [jnp.zeros((2, LANES), F32)]
+                site = site + jnp.dot(
+                    jnp.concatenate(picked, axis=0),
+                    hit[s],
+                    precision=HIGHEST,
+                    preferred_element_type=F32,
+                )
+            site_a[...] = jnp.concatenate([site[:, :LANES], site[:, LANES:]], axis=0)
         source, target = xs[k], xs[k + 1]
 
         def strip_divergence(i, carry, k=k, source=source):
@@ -410,35 +491,6 @@
         sums = lax.fori_loop(0, WIDE - 4 - 4 * k, strip_image, sums, unroll=IMG_UNROLL[k])
     strips = sums
 
-    def exchange(source, slots, partners, own, send_sems, recv_sems):
-        copies = []
-        for k, partner in enumerate(partners):
-            copy = pltpu.make_async_remote_copy(
-                src_ref=source,
-                dst_ref=slots.at[own],
-                send_sem=send_sems.at[k],
-                recv_sem=recv_sems.at[k],
-                device_id=partner,
-                device_id_type=MESH,
-            )
-            copy.start()
-            copies.append(copy)
-        slots[own] = source[...]
-        return copies
-
-    def tree(parts, join):
-        while len(parts) > 1:
-            joined = [join(parts[i], parts[i + 1]) for i in range(0, len(parts) - 1, 2)]
-            parts = joined + parts[len(parts) - len(parts) % 2 :]
-        return parts[0]
-
-    def join(p, q):
-        hi, more = two_sum(p[0], q[0])
-        return hi, p[1] + q[1] + more
-
-    def total(slots, number):
-        return tree([(slots[i, 0:8], slots[i, 8:16]) for i in range(number)], join)
-
     head, rest = [], []
     for n in range(6):
         hi, lo = two_sum(moments[n], strips[n])
@@ -448,79 +500,47 @@
         head.append(hi[0:1])
         rest.append(lo[0:1])
     blank = [jnp.zeros((2, LANES), F32)]
-    part_a[...] = jnp.concatenate(head + blank + rest + blank, axis=0)
-    copies = list(halos)
-    copies_a = exchange(part_a, slots_a, group_a, at_xs, a_send, a_recv)
-
-    edge_rows = 16 * PAIRS
-    lanes = lax.broadcasted_iota(jnp.int32, (LANES, LANES), 1)
-    outer = (lanes < HALO) | (lanes >= LANES - HALO)
-    mains = (v1, v2, None)
-    outs = (out1_ref, out2_ref, out3_ref)
-
-    def back_edges(i, carry, ks=(0, 1, 2)):
-        for k in ks:
-            for c in range(3):
-                even, odd = rows(xs[k + 1].at[c], (i + HALO) * SECTION)
-                first, second = mix(even, odd)
-                slot = (k * 3 + c) * edge_rows
-                back[pl.ds(slot + (8 + i) * PAIRS, PAIRS)] = first
-                back[pl.ds(slot + (2 + i) * PAIRS, PAIRS)] = second
-        return carry
-
-    def merge(k, c, t):
-        slot = (k * 3 + c) * edge_rows + t
-        edge = jnp.concatenate(
-            [
-                back[pl.ds(slot + 8 * PAIRS, 8, stride=PAIRS), :],
-                jnp.zeros((LANES - 16, LANES), F32),
-                back[pl.ds(slot, 8, stride=PAIRS), :],
-            ],
-            axis=0,
-        ).T
-        if k < 2:
-            main = jnp.concatenate(
-                [mains[k][c, pl.ds((2 * t + 1 + e) * PITCH, NS)] for e in range(2)], axis=0
-            )
-        else:
-            main = out3_ref[c, pl.ds(t * LANES, LANES)]
-        outs[k][c, pl.ds(t * LANES, LANES)] = jnp.where(outer, edge, main)
-
-    for slot in range(9):
-        for r in (0, 1, 14, 15):
-            back[pl.ds(slot * edge_rows + r * PAIRS, PAIRS)] = jnp.zeros((PAIRS, LANES), F32)
-    lax.fori_loop(0, HALO, back_edges, 0, unroll=HALO)
-    for k in (0, 1):
-        for c in (0, 1):
-            merge(k, c, 0)
-
-    site = jnp.zeros((8, 2 * LANES), F32)
-    for s, across in ((0, NS // 4), (1, 3 * NS // 4)):
-        picked = [v0[c, pl.ds(PITCH + across, 1)] for c in (0, 1)]
-        picked += [out1_ref[c, pl.ds(across, 1)] for c in (0, 1)]
-        picked += [out2_ref[c, pl.ds(across, 1)] for c in (0, 1)]
-        picked += [jnp.zeros((2, LANES), F32)]
-        site = site + jnp.dot(
-            jnp.concatenate(picked, axis=0),
-            hit[s],
-            precision=HIGHEST,
-            preferred_element_type=F32,
-        )
-    site_a[...] = jnp.concatenate([site[:, :LANES], site[:, LANES:]], axis=0)
-    copies_sa = exchange(site_a, site_slots_a, group_a, at_xs, site_a_send, site_a_recv)
+    hi, lo = jnp.concatenate(head + blank, axis=0), jnp.concatenate(rest + blank, axis=0)
+    for shift in (64, 32, 16, 8, 4, 2, 1):
+        hi, more = two_sum(hi, pltpu.roll(hi, shift, 1))
+        lo = lo + pltpu.roll(lo, shift, 1) + more
+    hi, lo = two_sum(hi, lo)
+    sublane = lax.broadcasted_iota(jnp.int32, (8, LANES), 0)
+    at_hi, at_lo = lane == sublane, lane == sublane + 8
+    packed = jnp.sum(jnp.where(at_hi, hi, 0.0) + jnp.where(at_lo, lo, 0.0), axis=0, keepdims=True)
+    part[...] = packed
+
+    copies = exchange(site_a, site_slots_a, group_a, at_xs, site_a_send, site_a_recv)
+    copies_a = copies
+
+    pl.semaphore_wait(ready, len(group_a))
+    ring = lambda a, n: min(a, n - a)
+    far = lambda o: -(ring(o[0] // 4, 4) + ring(o[0] % 4, 4) + ring(o[1] // 2, 4))
+    offsets = [(a, b) for a in range(len_size) for b in range(xs_size) if a or b]
+    lens = [lax.rem(at_len + a, len_size) for a in range(len_size)]
+    spots = [lax.rem(at_xs + b, xs_size) for b in range(xs_size)]
+    for a, b in sorted(offsets, key=far):
+        pltpu.make_async_remote_copy(
+            src_ref=part,
+            dst_ref=slots.at[pl.ds(me, 1)],
+            send_sem=all_send,
+            recv_sem=all_recv,
+            device_id=(lens[a], spots[b]),
+            device_id_type=MESH,
+        ).start()
+    slots[pl.ds(me, 1)] = part[...]
+
+    for i in range(HALO):
+        back_edges(i, 0, (2,))
+    merge(0, 2, 0)
+    merge(1, 2, 0)
+    for c in range(3):
+        merge(2, c, 0)
 
     for copy in copies_a:
         copy.wait_recv()
-    part_b[...] = jnp.concatenate(total(slots_a, xs_size), axis=0)
-    copies_b = exchange(part_b, slots_b, group_b, at_len, b_send, b_recv)
-
-    for copy in copies_sa:
-        copy.wait_recv()
     site_b[...] = tree([site_slots_a[i] for i in range(xs_size)], jnp.add)
-    copies_sb = exchange(site_b, site_slots_b, group_b, at_len, site_b_send, site_b_recv)
-
-    for k, c in ((0, 2), (1, 2), (2, 0), (2, 1), (2, 2)):
-        merge(k, c, 0)
+    copies_b = exchange(site_b, site_slots_b, group_b, at_len, site_b_send, site_b_recv)
 
     def merge_rest(t, carry):
         for k in range(3):
@@ -530,16 +550,40 @@
 
     lax.fori_loop(1, PAIRS, merge_rest, 0)
 
-    for copy in copies_b:
-        copy.wait_recv()
-    increment, solved = steps(*total(slots_b, len_size))
+    others = slots.at[pl.ds(0, count - 1)]
+    pltpu.make_async_copy(others, others, all_recv).wait()
+    hi, lo = tree(
+        [(slots[pl.ds(8 * i, 8)], jnp.zeros((8, LANES), F32)) for i in range(count // 8)], join
+    )
+    for shift in (4, 2, 1):
+        hi, more = two_sum(hi, pltpu.roll(hi, shift, 0))
+        lo = lo + pltpu.roll(lo, shift, 0) + more
+    pick = lambda mask, x: jnp.broadcast_to(
+        jnp.sum(jnp.where(mask, x, 0.0), axis=1, keepdims=True), (8, LANES)
+    )
+    increment, solved = steps(pick(at_hi, hi), pick(at_lo, hi) + pick(at_hi, lo))
     coefficients_ref[...] = jnp.concatenate(
         list(increment) + list(solved) + [jnp.zeros((1, LANES), F32)], axis=0
     )
-    for copy in copies_sb:
+
+    def combine(d, carry):
+        at = pl.ds(pl.multiple_of(d * NS, NS), NS)
+        for c in range(3):
+            p0 = v0[c, pl.ds((d + 1) * PITCH, NS)]
+            p1, p2, p3 = out1_ref[c, at], out2_ref[c, at], out3_ref[c, at]
+            inc_ref[c, at] = increment[0] * p0 + increment[1] * p1 + increment[2] * p2
+            solved_ref[c, at] = (
+                solved[0] * p0 + solved[1] * p1 + solved[2] * p2 + solved[3] * p3
+            )
+        return carry
+
+    lax.fori_loop(0, DEPTH, combine, 0)
+
+    for copy in copies_b:
         copy.wait_recv()
     sites_ref[...] = tree([site_slots_b[i] for i in range(len_size)], jnp.add)
-    for copy in halos + copies_a + copies_b + copies_sa + copies_sb:
+    pltpu.make_async_copy(others, others, all_send).wait()
+    for copy in halos + copies_a + copies_b:
         copy.wait_send()
 
 
@@ -603,10 +647,8 @@
 
 
 def finish_kernel(
-    b_ref,
-    v1_ref,
-    v2_ref,
-    v3_ref,
+    increment_ref,
+    solved_ref,
     coefficients_ref,
     sites_ref,
     spans_ref,
@@ -616,40 +658,27 @@
     inc_ref,
     res_ref,
     friction_ref,
-    x,
-    r,
+    first,
     out_sem,
 ):
+    rows = DEPTH * NS
+    at, top = pl.ds(NS, rows - NS), pl.ds(0, NS)
+    stores = []
+
+    def store(source, target):
+        copy = pltpu.make_async_copy(source, target, out_sem.at[len(stores)])
+        copy.start()
+        stores.append(copy)
+
+    for c in range(3):
+        store(increment_ref.at[c], inc_ref.at[c])
+        store(solved_ref.at[c, at], res_ref.at[c, at])
+
     me = lax.axis_index("len") * lax.axis_size("xs") + lax.axis_index("xs")
-    row = lambda n: coefficients_ref[pl.ds(n, 1)]
-    x0, x1, x2 = row(0), row(1), row(2)
-    stores = []
-
-    def combine(c, at):
-        p0, p1, p2, p3 = b_ref[c, at], v1_ref[c, at], v2_ref[c, at], v3_ref[c, at]
-        x[c, at] = x0 * p0 + x1 * p1 + x2 * p2
-        r[c, at] = row(3) * p0 + row(4) * p1 + row(5) * p2 + row(6) * p3
-
-    def store(c, at):
-        for ref, dst in ((x, inc_ref), (r, res_ref)):
-            copy = pltpu.make_async_copy(ref.at[c, at], dst.at[c, at], out_sem.at[len(stores)])
-            copy.start()
-            stores.append(copy)
-
-    rows = DEPTH * NS
-    for c in range(3):
-        for first, last in ((NS, rows // 2), (rows // 2, rows)):
-
-            def body(i, carry, c=c, first=first):
-                combine(c, pl.ds(pl.multiple_of(first + i * NS, NS), NS))
-                return carry
-
-            lax.fori_loop(0, (last - first) // NS, body, 0)
-            store(c, pl.ds(first, last - first))
-
-    wide = lambda a: jnp.concatenate([a, a], axis=1)
+
+    wide = lambda n: jnp.concatenate([coefficients_ref[pl.ds(n, 1)]] * 2, axis=1)
     site = jnp.concatenate([sites_ref[0:8], sites_ref[8:16]], axis=1)
-    readout = wide(x0) * site[0:2] + wide(x1) * site[2:4] + wide(x2) * site[4:6]
+    readout = wide(0) * site[0:2] + wide(1) * site[2:4] + wide(2) * site[4:6]
     radius = jnp.where(stick_ref[...] == 1, static_friction, kinetic_friction) * load_ref[...]
     trial = prior_ref[...] + elastic_stiffness * readout
     magnitude = jnp.sqrt(trial[0:1] * trial[0:1] + trial[1:2] * trial[1:2])
@@ -672,21 +701,22 @@
         for hit in hits
     ]
     for c in range(3):
-        combine(c, pl.ds(0, NS))
+        first[c] = solved_ref[c, top]
         for s, across in ((0, NS // 4), (1, 3 * NS // 4)):
-            at = pl.ds(across, 1)
+            node = pl.ds(across, 1)
             if c < 2:
                 drop = placed[s][c : c + 1]
             else:
-                drop = vertical_stiffness * x[c, at] * placed[s][2:3]
-            r[c, at] = r[c, at] - drop
-        store(c, pl.ds(0, NS))
+                drop = vertical_stiffness * increment_ref[c, node] * placed[s][2:3]
+            first[c, node] = first[c, node] - drop
+        store(first.at[c], res_ref.at[c, top])
     for copy in stores:
         copy.wait()
 
 
 def shards(right_side, mass_field, span_lengths, stick_flags, normal_load, prior_friction):
     sizes = (lax.axis_size("len"), lax.axis_size("xs"))
+    count = sizes[0] * sizes[1]
     rows = DEPTH * NS
     field = (3, rows, LANES)
     b = right_side.reshape(field)
@@ -698,14 +728,15 @@
     hbm = pl.BlockSpec(memory_space=pltpu.HBM)
     far = lambda a: pltpu.with_memory_space_constraint(a, pltpu.HBM)
     vmem = pl.BlockSpec(memory_space=pltpu.VMEM)
-    v0, v1, v2, v3, coefficients, sites = pl.pallas_call(
+    increment, solved, coefficients, sites = pl.pallas_call(
         lambda *refs: krylov_kernel(sizes, *refs),
         name="krylov",
-        out_shape=[pltpu.VMEM(field, F32)] * 4
+        out_shape=[pltpu.VMEM(field, F32)] * 2
         + [pltpu.VMEM((8, LANES), F32), pltpu.VMEM((16, LANES), F32)],
         in_specs=[hbm] * 3,
-        out_specs=[vmem] * 6,
+        out_specs=[vmem] * 4,
         scratch_shapes=[pltpu.VMEM((3, PADDED, LANES), F32)] * 3
+        + [pltpu.VMEM(field, F32)] * 3
         + [pltpu.VMEM((rows, LANES), F32), pltpu.VMEM((PADDED, LANES), F32)]
         + [pltpu.VMEM((3, STRIP, LANES), F32)] * 4
         + [pltpu.VMEM((STRIP, LANES), F32)] * 2
@@ -716,14 +747,12 @@
             pltpu.VMEM((2, LANES, 2 * LANES), F32),
             pltpu.VMEM(spans.shape, jnp.int32),
         ]
+        + [pltpu.VMEM((1, LANES), F32), pltpu.VMEM((count, LANES), F32)]
         + [pltpu.VMEM((16, LANES), F32)] * 2
         + [pltpu.VMEM((n, 16, LANES), F32) for n in (sizes[1], sizes[0])]
-        + [pltpu.VMEM((16, LANES), F32)] * 2
-        + [pltpu.VMEM((n, 16, LANES), F32) for n in (sizes[1], sizes[0])]
-        + [
-            pltpu.SemaphoreType.DMA((n,))
-            for n in (6, 2, 2) + 2 * (sizes[1], sizes[1], sizes[0], sizes[0])
-        ],
+        + [pltpu.SemaphoreType.DMA((n,)) for n in (5, 2, 2)]
+        + [pltpu.SemaphoreType.DMA, pltpu.SemaphoreType.DMA, pltpu.SemaphoreType.REGULAR]
+        + [pltpu.SemaphoreType.DMA((n,)) for n in (sizes[1], sizes[1], sizes[0], sizes[0])],
         compiler_params=pltpu.CompilerParams(
             collective_id=0, has_side_effects=True, vmem_limit_bytes=32 * 2**20
         ),
@@ -736,15 +765,14 @@
             jax.ShapeDtypeStruct(field, F32),
             jax.ShapeDtypeStruct(prior_friction.shape, F32),
         ],
-        in_specs=[vmem] * 10,
+        in_specs=[vmem] * 8,
         out_specs=[anywhere, anywhere, vmem],
         scratch_shapes=[
-            pltpu.VMEM(field, F32),
-            pltpu.VMEM(field, F32),
-            pltpu.SemaphoreType.DMA((18,)),
+            pltpu.VMEM((3, NS, LANES), F32),
+            pltpu.SemaphoreType.DMA((9,)),
         ],
         compiler_params=pltpu.CompilerParams(vmem_limit_bytes=24 * 2**20),
-    )(v0, v1, v2, v3, coefficients, sites, spans, stick, load, prior_friction)
+    )(increment, solved, coefficients, sites, spans, stick, load, prior_friction)
     return (
         increment.reshape(right_side.shape),
         residual.reshape(right_side.shape),

time: 29.2 us -> 28 us (0.959)
  Pallas kernels: 28.3 us -> 27.2 us
    pallas_call x1, Pallas kernels: 25.5 us -> 24.9 us  [shards(): pl.pallas_call(lambda *refs: krylov_kernel(sizes, *refs), name='krylov',...]
    pallas_call x1, Pallas kernels: 2.79 us -> 2.33 us  [shards(): pl.pallas_call(finish_kernel, name='finish', out_shape=[jax.ShapeDtypeStr...]
where the time goes in v5:
time: 28 us; the launch traced here: 27.9 us
  Pallas kernels  27.2 us (97%)
  between operations  0.7 us (2%)
    pallas_call x1, Pallas kernels, shards(): pl.pallas_call(lambda *refs: krylov_kernel(sizes, *refs), name='krylov',...  24.9 us
    pallas_call x1, Pallas kernels, shards(): pl.pallas_call(finish_kernel, name='finish', out_shape=[jax.ShapeDtypeStr...  2.33 us

profile of v5, /device:TPU:1, one launch (start us, length us, event | category | flops | bytes accessed | tf_op | source)
XLA Modules:
  0.0 27.9 jit_solution(5350852331393187102)
XLA Ops:
  0.6 0.0 copy-start
  0.6 0.0 copy-start.3
  0.7 0.0 copy-start.2
  0.7 0.0 copy-start.1
  0.7 24.9 %krylov.1 = (f32[3,1024,128]{2,1,0:T(8,128)S(1)}, f32[3,1024,128]{2,1,0:T(8,128)S(1)}, f32[8,128]{1,0:T(8,128)S(1)}, f32[16,128]{1,0:T(8,128)S(1)}) custom-call(f32[3,1024,128]{2,1,0:T(8,128)} %bitcast.11, f32[1024,128]{1,0:T(8,128)} %bitcast.12, s32[1,128]{1,0:T(1,128)} %bitcast.7), custom_call_target="tpu_custom_call" | custom-call | tf_op jit(solution)/shard_map/krylov/pallas_call | solution.py:731
  25.5 0.0 copy-done
  25.6 0.0 copy-done.3
  25.6 0.0 copy-done.2
  25.6 0.0 copy-done.1
  25.6 2.3 %finish.1 = (f32[3,1024,128]{2,1,0:T(8,128)}, f32[3,1024,128]{2,1,0:T(8,128)}, f32[2,256]{1,0:T(2,128)}) custom-call(f32[3,1024,128]{2,1,0:T(8,128)S(1)} %get-tuple-element.10.increment_ref, f32[3,1024,128]{2,1,0:T(8,128)S(1)} %get-tuple-element.11.solved_ref, f32[8,128]{1,0:T(8,128)S(1)} %get-tuple-element.12.coefficients_ref, ...), custom_call_target="tpu_custom_call" | custom-call | tf_op jit(solution)/shard_map/finish/pallas_call | solution.py:760
Async XLA Ops:
  0.6 24.9 %copy-start = (f32[2,256]{1,0:T(2,128)S(1)}, f32[2,256]{1,0:T(2,128)}, u32[]{:S(2)}) copy-start(f32[2,256]{1,0:T(2,128)} %prior_ref.1) | copy-start | bytes 6148
  0.6 24.9 %copy-start.3 = (f32[256]{0:T(256)S(1)}, f32[256]{0:T(256)}, u32[]{:S(2)}) copy-start(f32[256]{0:T(256)} %param.10) | copy-start | bytes 3076
  0.7 24.9 %copy-start.2 = (s32[256]{0:T(256)S(1)}, s32[256]{0:T(256)}, u32[]{:S(2)}) copy-start(s32[256]{0:T(256)} %param.9) | copy-start | bytes 3076
  0.7 24.9 %copy-start.1 = (s32[128]{0:T(128)S(1)}, s32[128]{0:T(128)}, u32[]{:S(2)}) copy-start(s32[128]{0:T(128)} %param.8) | copy-start | bytes 1540

commit v6 on v5

--- a/solution.py
+++ b/solution.py
@@ -125,6 +125,11 @@
     group_a = [(at_len, lax.rem(at_xs + k, xs_size)) for k in range(1, xs_size)]
     group_b = [(lax.rem(at_len + k, len_size), at_xs) for k in range(1, len_size)]
 
+    barrier = pltpu.get_barrier_semaphore()
+    partners = [place(left), place(right)] + group_b + group_a
+    for partner in partners:
+        pl.semaphore_signal(barrier, inc=1, device_id=partner, device_id_type=MESH)
+
     spans_copy = pltpu.make_async_copy(spans_ref, spans, in_sem.at[4])
     spans_copy.start()
     for c in range(3):
@@ -139,11 +144,6 @@
 
         lax.fori_loop(0, DEPTH, load, 0)
     pltpu.make_async_copy(mass_ref, mass, in_sem.at[3]).start()
-
-    barrier = pltpu.get_barrier_semaphore()
-    partners = [place(left), place(right)] + group_b + group_a
-    for partner in partners:
-        pl.semaphore_signal(barrier, inc=1, device_id=partner, device_id_type=MESH)
 
     def guard(d, carry):
         row = (d + 1) * PITCH + NS

time: 28 us -> 27.7 us (0.989)
  Pallas kernels: 27.2 us -> 26.8 us
    pallas_call x1, Pallas kernels: 24.9 us -> 24.5 us  [shards(): pl.pallas_call(lambda *refs: krylov_kernel(sizes, *refs), name='krylov',...]
where the time goes in v6:
time: 27.7 us; the launch traced here: 27.6 us
  Pallas kernels  26.8 us (97%)
  between operations  0.7 us (3%)
    pallas_call x1, Pallas kernels, shards(): pl.pallas_call(lambda *refs: krylov_kernel(sizes, *refs), name='krylov',...  24.5 us
    pallas_call x1, Pallas kernels, shards(): pl.pallas_call(finish_kernel, name='finish', out_shape=[jax.ShapeDtypeStr...  2.33 us

profile of v6, /device:TPU:1, one launch (start us, length us, event | category | flops | bytes accessed | tf_op | source)
XLA Modules:
  0.0 27.6 jit_solution(12579422518852701591)
XLA Ops:
  0.6 0.0 copy-start
  0.6 0.0 copy-start.3
  0.7 0.0 copy-start.2
  0.7 0.0 copy-start.1
  0.7 24.5 %krylov.1 = (f32[3,1024,128]{2,1,0:T(8,128)S(1)}, f32[3,1024,128]{2,1,0:T(8,128)S(1)}, f32[8,128]{1,0:T(8,128)S(1)}, f32[16,128]{1,0:T(8,128)S(1)}) custom-call(f32[3,1024,128]{2,1,0:T(8,128)} %bitcast.11, f32[1024,128]{1,0:T(8,128)} %bitcast.12, s32[1,128]{1,0:T(1,128)} %bitcast.7), custom_call_target="tpu_custom_call" | custom-call | tf_op jit(solution)/shard_map/krylov/pallas_call | solution.py:731
  25.2 0.0 copy-done
  25.2 0.0 copy-done.3
  25.2 0.0 copy-done.2
  25.2 0.0 copy-done.1
  25.2 2.3 %finish.1 = (f32[3,1024,128]{2,1,0:T(8,128)}, f32[3,1024,128]{2,1,0:T(8,128)}, f32[2,256]{1,0:T(2,128)}) custom-call(f32[3,1024,128]{2,1,0:T(8,128)S(1)} %get-tuple-element.10.increment_ref, f32[3,1024,128]{2,1,0:T(8,128)S(1)} %get-tuple-element.11.solved_ref, f32[8,128]{1,0:T(8,128)S(1)} %get-tuple-element.12.coefficients_ref, ...), custom_call_target="tpu_custom_call" | custom-call | tf_op jit(solution)/shard_map/finish/pallas_call | solution.py:760
Async XLA Ops:
  0.6 24.6 %copy-start = (f32[2,256]{1,0:T(2,128)S(1)}, f32[2,256]{1,0:T(2,128)}, u32[]{:S(2)}) copy-start(f32[2,256]{1,0:T(2,128)} %prior_ref.1) | copy-start | bytes 6148
  0.6 24.6 %copy-start.3 = (f32[256]{0:T(256)S(1)}, f32[256]{0:T(256)}, u32[]{:S(2)}) copy-start(f32[256]{0:T(256)} %param.10) | copy-start | bytes 3076
  0.7 24.6 %copy-start.2 = (s32[256]{0:T(256)S(1)}, s32[256]{0:T(256)}, u32[]{:S(2)}) copy-start(s32[256]{0:T(256)} %param.9) | copy-start | bytes 3076
  0.7 24.6 %copy-start.1 = (s32[128]{0:T(128)S(1)}, s32[128]{0:T(128)}, u32[]{:S(2)}) copy-start(s32[128]{0:T(128)} %param.8) | copy-start | bytes 1540

commit v7 on v6

--- a/solution.py
+++ b/solution.py
@@ -26,9 +26,9 @@
 OWN = 2 * HALO * 4 * PAIRS
 LANDED = HALO * 4 * PAIRS
 
-UNROLL = 4
+UNROLL = 8
 DIV_UNROLL = (16, 12, 8)
-IMG_UNROLL = (7, 5, 6)
+IMG_UNROLL = (14, 10, 6)
 
 MESH = pl.DeviceIdType.MESH
 HIGHEST = lax.Precision.HIGHEST

time: 27.7 us -> 27.2 us (0.982)
  Pallas kernels: 26.8 us -> 26.3 us
    pallas_call x1, Pallas kernels: 24.5 us -> 24 us  [shards(): pl.pallas_call(lambda *refs: krylov_kernel(sizes, *refs), name='krylov',...]
where the time goes in v7:
time: 27.2 us; the launch traced here: 27 us
  Pallas kernels  26.3 us (97%)
  between operations  0.7 us (3%)
    pallas_call x1, Pallas kernels, shards(): pl.pallas_call(lambda *refs: krylov_kernel(sizes, *refs), name='krylov',...  24 us
    pallas_call x1, Pallas kernels, shards(): pl.pallas_call(finish_kernel, name='finish', out_shape=[jax.ShapeDtypeStr...  2.33 us

profile of v7, /device:TPU:1, one launch (start us, length us, event | category | flops | bytes accessed | tf_op | source)
XLA Modules:
  0.0 27.0 jit_solution(6722739336347041541)
XLA Ops:
  0.6 0.0 copy-start
  0.6 0.0 copy-start.3
  0.7 0.0 copy-start.2
  0.7 0.0 copy-start.1
  0.7 24.0 %krylov.1 = (f32[3,1024,128]{2,1,0:T(8,128)S(1)}, f32[3,1024,128]{2,1,0:T(8,128)S(1)}, f32[8,128]{1,0:T(8,128)S(1)}, f32[16,128]{1,0:T(8,128)S(1)}) custom-call(f32[3,1024,128]{2,1,0:T(8,128)} %bitcast.11, f32[1024,128]{1,0:T(8,128)} %bitcast.12, s32[1,128]{1,0:T(1,128)} %bitcast.7), custom_call_target="tpu_custom_call" | custom-call | tf_op jit(solution)/shard_map/krylov/pallas_call | solution.py:731
  24.7 0.0 copy-done
  24.7 0.0 copy-done.3
  24.7 0.0 copy-done.2
  24.7 0.0 copy-done.1
  24.7 2.3 %finish.1 = (f32[3,1024,128]{2,1,0:T(8,128)}, f32[3,1024,128]{2,1,0:T(8,128)}, f32[2,256]{1,0:T(2,128)}) custom-call(f32[3,1024,128]{2,1,0:T(8,128)S(1)} %get-tuple-element.10.increment_ref, f32[3,1024,128]{2,1,0:T(8,128)S(1)} %get-tuple-element.11.solved_ref, f32[8,128]{1,0:T(8,128)S(1)} %get-tuple-element.12.coefficients_ref, ...), custom_call_target="tpu_custom_call" | custom-call | tf_op jit(solution)/shard_map/finish/pallas_call | solution.py:760
Async XLA Ops:
  0.6 24.1 %copy-start = (f32[2,256]{1,0:T(2,128)S(1)}, f32[2,256]{1,0:T(2,128)}, u32[]{:S(2)}) copy-start(f32[2,256]{1,0:T(2,128)} %prior_ref.1) | copy-start | bytes 6148
  0.6 24.1 %copy-start.3 = (f32[256]{0:T(256)S(1)}, f32[256]{0:T(256)}, u32[]{:S(2)}) copy-start(f32[256]{0:T(256)} %param.10) | copy-start | bytes 3076
  0.7 24.1 %copy-start.2 = (s32[256]{0:T(256)S(1)}, s32[256]{0:T(256)}, u32[]{:S(2)}) copy-start(s32[256]{0:T(256)} %param.9) | copy-start | bytes 3076
  0.7 24.1 %copy-start.1 = (s32[128]{0:T(128)S(1)}, s32[128]{0:T(128)}, u32[]{:S(2)}) copy-start(s32[128]{0:T(128)} %param.8) | copy-start | bytes 1540
